TPU v7x, 32 devices: a whole 2x2x4 slice. The times are simulated.
32 devices in a mesh: dp: 16 (over z, y, x), role: 2 (over core).
Axes of the slice: x: 2, y: 2, z: 4, core: 2. Of those that a mesh axis runs over, the one named last changes fastest.
Arguments:
- frames: bfloat16 [16, 768, 1024], P('dp', 'role'), may hold values from -6 to 6
- frames_cotangent: bfloat16 [16, 768, 1024], P('dp', 'role'), may hold values from -6 to 6
- phoneme_len: int32 [16], P('dp'), may hold values from 1 to 96, as said below
- prompt_len: int32 [16], P('dp'), may hold values from 96 to 288, as said below
- target_segment: int32 [16, 384], P('dp'), may hold values from 0 to 3, never falling along the last dimension, each value on 1 to 192 neighbouring positions
- first_gain: bfloat16 [1024], P(('dp', 'role')), may hold values from 0.5 to 1.5
- first_shift: bfloat16 [1024], P(('dp', 'role')), may hold values from -1.5 to 1.5
- inward_weight: bfloat16 [1024, 3072], P(('dp', 'role')), may hold values from -0.1875 to 0.1875
- query_bias: bfloat16 [1024], P(('dp', 'role')), may hold values from -2.5 to 2.5
- value_bias: bfloat16 [1024], P(('dp', 'role')), may hold values from -0.25 to 0.25
- outward_weight: bfloat16 [1024, 1024], P(('dp', 'role')), may hold values from -2 to 2
- outward_bias: bfloat16 [1024], P(('dp', 'role')), may hold values from -2.5 to 2.5
- second_gain: bfloat16 [1024], P(('dp', 'role')), may hold values from 0.5 to 1.5
- second_shift: bfloat16 [1024], P(('dp', 'role')), may hold values from -1.5 to 1.5
- expand_weight: bfloat16 [1024, 4096], P(('dp', 'role')), may hold values from -0.1875 to 0.1875
- expand_bias: bfloat16 [4096], P(('dp', 'role')), may hold values from -2.5 to 2.5
- reduce_weight: bfloat16 [4096, 1024], P(('dp', 'role')), may hold values from -0.09375 to 0.09375
- reduce_bias: bfloat16 [1024], P(('dp', 'role')), may hold values from -2.5 to 2.5
Outputs:
- result: bfloat16 [16, 768, 1024], P('dp', 'role')
- frames_gradient: bfloat16 [16, 768, 1024], P('dp', 'role')
- first_gain_gradient: float32 [1024], P(('dp', 'role'))
- first_shift_gradient: float32 [1024], P(('dp', 'role'))
- inward_weight_gradient: float32 [1024, 3072], P(('dp', 'role'))
- query_bias_gradient: float32 [1024], P(('dp', 'role'))
- value_bias_gradient: float32 [1024], P(('dp', 'role'))
- outward_weight_gradient: float32 [1024, 1024], P(('dp', 'role'))
- outward_bias_gradient: float32 [1024], P(('dp', 'role'))
- second_gain_gradient: float32 [1024], P(('dp', 'role'))
- second_shift_gradient: float32 [1024], P(('dp', 'role'))
- expand_weight_gradient: float32 [1024, 4096], P(('dp', 'role'))
- expand_bias_gradient: float32 [4096], P(('dp', 'role'))
- reduce_weight_gradient: float32 [4096, 1024], P(('dp', 'role'))
- reduce_bias_gradient: float32 [1024], P(('dp', 'role'))
Inputs may be any that keep to these rules, and one draw needn't show every extreme that they name: In some group phoneme_len + prompt_len equals 384; in some group phoneme_len is 1. phoneme_len + prompt_len never exceeds 384. `target_segment`: each group's target rows hold 4 utterances in order, each of at most 192 rows.
All inputs are finite; a program needn't handle non-finite values.
Results may differ from a plain program's by a relative error of at most 0.014.
Values may be sent and summed in bfloat16 or wider, within the bound.
A program may use at most 256 MiB of HBM per device.

v0:
```python
import jax
import jax.numpy as jnp
from jax import lax
from jax.sharding import PartitionSpec as P

D = 1024
H = 16
HD = 64


EPS = 1e-05
MASKED = -1e30


def passed_along(block, axis, distance):
    devices = range(lax.axis_size(axis))
    route = [(i - distance, i) for i in devices if i - distance in devices]
    return lax.ppermute(block, axis, route)


def normalize(values, gain, shift):
    mean_value = jnp.mean(values, axis=-1, keepdims=True)
    centered = values - mean_value
    spread = jnp.mean(centered * centered, axis=-1, keepdims=True)
    return centered * lax.rsqrt(spread + EPS) * gain + shift


def smooth_gate(values):
    return jax.nn.gelu(values, approximate=False)


def inner_rows(left, right):
    return lax.dot_general(
        left, right, (((0,), (0,)), ((), ())), preferred_element_type=jnp.float32
    )


def outer_cols(left, right):
    return lax.dot_general(
        left, right, (((1,), (1,)), ((), ())), preferred_element_type=jnp.float32
    )


def shards(
    frames,
    frames_cotangent,
    phoneme_len,
    prompt_len,
    target_segment,
    first_gain,
    first_shift,
    inward_weight,
    query_bias,
    value_bias,
    outward_weight,
    outward_bias,
    second_gain,
    second_shift,
    expand_weight,
    expand_bias,
    reduce_weight,
    reduce_bias,
):
    attention_part = (
        lax.all_gather(first_gain, ("dp", "role"), axis=0, tiled=True),
        lax.all_gather(first_shift, ("dp", "role"), axis=0, tiled=True),
        lax.all_gather(inward_weight, ("dp", "role"), axis=0, tiled=True),
        lax.all_gather(query_bias, ("dp", "role"), axis=0, tiled=True),
        lax.all_gather(value_bias, ("dp", "role"), axis=0, tiled=True),
        lax.all_gather(outward_weight, ("dp", "role"), axis=0, tiled=True),
        lax.all_gather(outward_bias, ("dp", "role"), axis=0, tiled=True),
    )
    (
        full_gain,
        full_shift,
        full_inward,
        full_query_bias,
        full_value_bias,
        full_outward,
        full_outward_bias,
    ) = attention_part
    side = lax.axis_index("role")
    local_rows = frames.shape[1]
    scale = HD ** (-0.5)
    current = frames[0].astype(jnp.float32)
    normed = normalize(
        current, full_gain.astype(jnp.float32), full_shift.astype(jnp.float32)
    ).astype(jnp.bfloat16)
    mixed = jnp.dot(normed, full_inward, preferred_element_type=jnp.float32)
    queries = (mixed[:, :D] + full_query_bias.astype(jnp.float32)).astype(jnp.bfloat16)
    keys_own = mixed[:, D : 2 * D].astype(jnp.bfloat16)
    values_own = (mixed[:, 2 * D :] + full_value_bias.astype(jnp.float32)).astype(jnp.bfloat16)
    remote_keys, remote_values = passed_along((keys_own, values_own), "role", 1)
    keys_all = jnp.concatenate([remote_keys, keys_own], axis=0)
    values_all = jnp.concatenate([remote_values, values_own], axis=0)
    row_index = jnp.arange(local_rows)[:, None]
    col_index = jnp.arange(2 * local_rows)[None, :]
    own_col = col_index - local_rows
    prefix_length = phoneme_len[0] + prompt_len[0]
    segment = target_segment[0]
    key_segment = jnp.concatenate([jnp.full((local_rows,), -1, jnp.int32), segment])
    prompt_rows = (own_col >= 0) & (own_col <= row_index) & (own_col < prefix_length)
    target_rows = (col_index < prefix_length) | (own_col >= 0) & (own_col <= row_index) & (
        key_segment[None, :] == segment[:, None]
    )
    allowed = jnp.where(side == 0, prompt_rows, target_rows)

    def attend(index):
        start = index * HD
        head_query = lax.dynamic_slice_in_dim(queries, start, HD, 1)
        head_key = lax.dynamic_slice_in_dim(keys_all, start, HD, 1)
        head_value = lax.dynamic_slice_in_dim(values_all, start, HD, 1)
        scores = outer_cols(head_query, head_key) * scale
        masked = jnp.where(allowed, scores, MASKED)
        peak = jnp.max(masked, axis=1, keepdims=True)
        expo = jnp.exp(masked - peak)
        total = jnp.sum(expo, axis=1, keepdims=True)
        probs = (expo / total).astype(jnp.bfloat16)
        return (
            jnp.dot(probs, head_value, preferred_element_type=jnp.float32),
            (peak + jnp.log(total))[:, 0],
        )

    head_outs, log_totals = lax.map(attend, jnp.arange(H))
    attended = head_outs.transpose(1, 0, 2).reshape(local_rows, D).astype(jnp.bfloat16)
    middle = (
        current
        + jnp.dot(attended, full_outward, preferred_element_type=jnp.float32)
        + full_outward_bias.astype(jnp.float32)
    )
    feed_part = (
        lax.all_gather(second_gain, ("dp", "role"), axis=0, tiled=True),
        lax.all_gather(second_shift, ("dp", "role"), axis=0, tiled=True),
        lax.all_gather(expand_weight, ("dp", "role"), axis=0, tiled=True),
        lax.all_gather(expand_bias, ("dp", "role"), axis=0, tiled=True),
        lax.all_gather(reduce_weight, ("dp", "role"), axis=0, tiled=True),
        lax.all_gather(reduce_bias, ("dp", "role"), axis=0, tiled=True),
    )
    full_gain_two, full_shift_two, full_expand, full_expand_bias, full_reduce, full_reduce_bias = (
        feed_part
    )
    gain_two = full_gain_two.astype(jnp.float32)
    shift_two = full_shift_two.astype(jnp.float32)
    normed_two = normalize(middle, gain_two, shift_two).astype(jnp.bfloat16)
    inner = jnp.dot(
        normed_two, full_expand, preferred_element_type=jnp.float32
    ) + full_expand_bias.astype(jnp.float32)
    active = smooth_gate(inner).astype(jnp.bfloat16)
    output = (
        middle
        + jnp.dot(active, full_reduce, preferred_element_type=jnp.float32)
        + full_reduce_bias.astype(jnp.float32)
    )
    result = output.astype(jnp.bfloat16)[None]
    again_expand = feed_part[2]
    again_reduce = feed_part[4]
    again_gain = attention_part[0].astype(jnp.float32)
    again_shift = attention_part[1].astype(jnp.float32)
    again_inward = attention_part[2]
    again_outward = attention_part[5]
    upstream = frames_cotangent[0]
    upstream_float = upstream.astype(jnp.float32)
    reduce_bias_term = jnp.sum(upstream_float, axis=0)
    reduce_weight_term = inner_rows(active, upstream)
    back_active = outer_cols(upstream, again_reduce)
    gate_pull = jax.vjp(smooth_gate, inner)[1]
    back_inner = gate_pull(back_active)[0].astype(jnp.bfloat16)
    expand_bias_term = jnp.sum(back_inner.astype(jnp.float32), axis=0)
    expand_weight_term = inner_rows(normed_two, back_inner)
    back_normed_two = outer_cols(back_inner, again_expand)
    second_pull = jax.vjp(normalize, middle, gain_two, shift_two)[1]
    middle_part, second_gain_term, second_shift_term = second_pull(back_normed_two)
    back_middle = upstream_float + middle_part
    back_branch = back_middle.astype(jnp.bfloat16)
    outward_bias_term = jnp.sum(back_branch.astype(jnp.float32), axis=0)
    outward_weight_term = inner_rows(attended, back_branch)
    back_attended = outer_cols(back_branch, again_outward).astype(jnp.bfloat16)

    def attend_back(inputs):
        index, log_total = inputs
        start = index * HD
        head_query = lax.dynamic_slice_in_dim(queries, start, HD, 1)
        head_key = lax.dynamic_slice_in_dim(keys_all, start, HD, 1)
        head_value = lax.dynamic_slice_in_dim(values_all, start, HD, 1)
        head_upstream = lax.dynamic_slice_in_dim(back_attended, start, HD, 1)
        scores = outer_cols(head_query, head_key) * scale
        probs = jnp.where(allowed, jnp.exp(scores - log_total[:, None]), 0.0)
        back_probs = outer_cols(head_upstream, head_value)
        centre = jnp.sum(probs * back_probs, axis=1, keepdims=True)
        back_scores = (probs * (back_probs - centre)).astype(jnp.bfloat16)
        back_query = jnp.dot(back_scores, head_key, preferred_element_type=jnp.float32) * scale
        back_key = inner_rows(back_scores, head_query) * scale
        back_value = inner_rows(probs.astype(jnp.bfloat16), head_upstream)
        return (back_query, back_key, back_value)

    head_query_grads, head_key_grads, head_value_grads = lax.map(
        attend_back, (jnp.arange(H), log_totals)
    )
    back_queries = head_query_grads.transpose(1, 0, 2).reshape(local_rows, D)
    back_keys_all = head_key_grads.transpose(1, 0, 2).reshape(2 * local_rows, D)
    back_values_all = head_value_grads.transpose(1, 0, 2).reshape(2 * local_rows, D)
    returned_keys, returned_values = (
        passed_along(back_keys_all[:local_rows].astype(jnp.bfloat16), "role", -1).astype(
            jnp.float32
        ),
        passed_along(back_values_all[:local_rows].astype(jnp.bfloat16), "role", -1).astype(
            jnp.float32
        ),
    )
    query_low = back_queries.astype(jnp.bfloat16)
    key_low = (back_keys_all[local_rows:] + returned_keys).astype(jnp.bfloat16)
    value_low = (back_values_all[local_rows:] + returned_values).astype(jnp.bfloat16)
    back_mixed = jnp.concatenate([query_low, key_low, value_low], axis=1)
    query_bias_term = jnp.sum(query_low.astype(jnp.float32), axis=0)
    value_bias_term = jnp.sum(value_low.astype(jnp.float32), axis=0)
    inward_weight_term = inner_rows(normed, back_mixed)
    back_normed = outer_cols(back_mixed, again_inward)
    first_pull = jax.vjp(normalize, current, again_gain, again_shift)[1]
    frame_part, first_gain_term, first_shift_term = first_pull(back_normed)
    frames_gradient = (back_middle + frame_part).astype(jnp.bfloat16)[None]
    totals = (
        lax.psum_scatter(first_gain_term, ("dp", "role"), scatter_dimension=0, tiled=True),
        lax.psum_scatter(first_shift_term, ("dp", "role"), scatter_dimension=0, tiled=True),
        lax.psum_scatter(inward_weight_term, ("dp", "role"), scatter_dimension=0, tiled=True),
        lax.psum_scatter(query_bias_term, ("dp", "role"), scatter_dimension=0, tiled=True),
        lax.psum_scatter(value_bias_term, ("dp", "role"), scatter_dimension=0, tiled=True),
        lax.psum_scatter(outward_weight_term, ("dp", "role"), scatter_dimension=0, tiled=True),
        lax.psum_scatter(outward_bias_term, ("dp", "role"), scatter_dimension=0, tiled=True),
        lax.psum_scatter(second_gain_term, ("dp", "role"), scatter_dimension=0, tiled=True),
        lax.psum_scatter(second_shift_term, ("dp", "role"), scatter_dimension=0, tiled=True),
        lax.psum_scatter(expand_weight_term, ("dp", "role"), scatter_dimension=0, tiled=True),
        lax.psum_scatter(expand_bias_term, ("dp", "role"), scatter_dimension=0, tiled=True),
        lax.psum_scatter(reduce_weight_term, ("dp", "role"), scatter_dimension=0, tiled=True),
        lax.psum_scatter(reduce_bias_term, ("dp", "role"), scatter_dimension=0, tiled=True),
    )
    return (
        result,
        frames_gradient,
        totals[0],
        totals[1],
        totals[2],
        totals[3],
        totals[4],
        totals[5],
        totals[6],
        totals[7],
        totals[8],
        totals[9],
        totals[10],
        totals[11],
        totals[12],
    )


def solution(mesh):
    placed = (
        P("dp", "role", None),
        P("dp", "role", None),
        P("dp"),
        P("dp"),
        P("dp", None),
        P(("dp", "role")),
        P(("dp", "role")),
        P(("dp", "role"), None),
        P(("dp", "role")),
        P(("dp", "role")),
        P(("dp", "role"), None),
        P(("dp", "role")),
        P(("dp", "role")),
        P(("dp", "role")),
        P(("dp", "role"), None),
        P(("dp", "role")),
        P(("dp", "role"), None),
        P(("dp", "role")),
    )
    return jax.shard_map(
        shards,
        mesh=mesh,
        in_specs=placed,
        out_specs=(
            P("dp", "role", None),
            P("dp", "role", None),
            P(("dp", "role")),
            P(("dp", "role")),
            P(("dp", "role"), None),
            P(("dp", "role")),
            P(("dp", "role")),
            P(("dp", "role"), None),
            P(("dp", "role")),
            P(("dp", "role")),
            P(("dp", "role")),
            P(("dp", "role"), None),
            P(("dp", "role")),
            P(("dp", "role"), None),
            P(("dp", "role")),
        ),
        check_vma=False,
    )
```

profile of v0, /device:TPU:1, one launch (start us, length us, event | category | flops | bytes accessed | tf_op | source)
XLA Modules:
  0.0 1038.8 jit_solution(551869251949099456)
XLA Ops:
  16.2 41.1 %all-reduce.19 = (bf16[1024]{0:T(1024)(128)(2,1)S(1)}, bf16[1024]{0:T(1024)(128)(2,1)S(1)}, bf16[1024]{0:T(1024)(128)(2,1)S(1)}, bf16[1024]{0:T(1024)(128)(2,1)S...) all-reduce(bf16[1024]{0:T(1024)(128)(2,1)S(1)} %dynamic-update-slic, ...), channel_id=1, replica_groups=mesh['dp'=16,'role'=2] {'dp','role'}, use_global_device_ids=true, to_apply=%add.2 | all-reduce | flops 8192 | bytes 32768
  59.0 24.0 %all-gather.6.cloned.1.call-done = bf16[1024,3072]{1,0:T(8,128)(2,1)} async-done(((bf16[32,3072]{1,0:T(8,128)(2,1)}), bf16[1024,3072]{1,0:T(8,128)(2,1)}) %all-gather.6.cloned.1.call-update) | async-done | bytes 6291472 | tf_op jit(solution)/shard_map/all_gather | solution.py:67
  83.0 4.9 fusion.89
  93.6 40.9 %all-gather = bf16[32,1,128]{2,1,0:T(2,128)(2,1)S(1)} all-gather(bf16[1,1,128]{2,1,0:T(2,128)(2,1)S(1)} %bitcast.140), channel_id=1, replica_groups=mesh['dp'=16,'role'=2] {'dp','role'}, dimensions={0}, use_global_device_ids=true | all-gather | bytes 8448 | tf_op jit(solution)/shard_map/all_gather | solution.py:135
  135.9 2.5 pad_maximum_fusion.1
  138.5 80.7 %while.28 = (s32[]{:T(128)}, bf16[16,384,64]{1,2,0:T(8,128)(2,1)S(1)}, f32[16,384]{1,0:T(8,128)S(1)}, s32[16]{0:T(128)S(1)}, bf16[384,1024]{1,0:T(8,128)(2,1)}, ...) while((s32[]{:T(128)}, ...), condition=%wide.region_5.6_spmd.clone, body=%wide.region_2.5_spmd.clone.sunk | while | flops 79920768 | bytes 4160487 | solution.py:124
  190.0 2.0 fusion.137
  219.2 2.7 fusion.99
  222.2 20.5 %multiply_convert_fusion.1 = (bf16[384,4096]{1,0:T(8,128)(2,1)}, f32[384,4096]{1,0:T(8,128)}, f32[384,4096]{1,0:T(8,128)}) fusion(f32[4096]{0:T(1024)S(1)} %bitcast.139, bf16[1024,4096]{1,0:T(8,128)(2,1)} %all-gather.10.cloned.1.call-done, f32[384,1024]{1,0:T(8,128)S(1)} %get-tuple-element.305, f32[1024]{0:T(1024)S(1)} %convert_element_type.145, ...), kind=kOutput, calls=%fused_computation.63 | convolution fusion | flops 3327000576 | bytes 25717760 | tf_op jit(solution)/shard_map/dot_general | solution.py:145
  242.7 56.2 %all-gather.12.cloned.1.call-done = bf16[4096,1024]{1,0:T(8,128)(2,1)} async-done(((bf16[128,1024]{1,0:T(8,128)(2,1)}), bf16[4096,1024]{1,0:T(8,128)(2,1)}) %all-gather.12.cloned.1.call-update) | async-done | bytes 8388624 | tf_op jit(solution)/shard_map/all_gather | solution.py:136
  298.9 11.0 %convert_reduce_fusion = (f32[4096]{0:T(1024)S(1)}, bf16[384,4096]{1,0:T(8,128)(2,1)S(1)}) fusion(f32[384,4096]{1,0:T(8,128)} %get-tuple-element.295, f32[384,4096]{1,0:T(8,128)} %get-tuple-element.306, bf16[4096,1024]{1,0:T(8,128)(2,1)} %all-gather.12.cloned.1.call-done, bf16[1,384,1024]{2,1,0:T(8,128)(2,1)} %param.23), kind=kOutput, calls=%fused_computation.61 | convolution fusion | flops 3246387200 | bytes 24920064 | tf_op jit(solution)/shard_map/dot_general | solution.py:39
  309.9 3.8 multiply_reduce_fusion.1
  316.5 3.4 fusion.100
  321.0 3.5 convolution_convert_fusion
  324.6 159.9 %while.29 = (s32[]{:T(128)}, bf16[16,384,64]{1,2,0:T(8,128)(2,1)S(1)}, f32[16,768,64]{1,2,0:T(8,128)}, f32[16,768,64]{1,2,0:T(8,128)}, s32[16]{0:T(128)S(1)}, /*...) while((s32[]{:T(128)}, ...), condition=%wide.region_12.13_spmd.clone, body=%wide.region_10.12_spmd.clone.sunk | while | flops 193535616 | bytes 10343943 | solution.py:196
  327.2 2.0 multiply_reduce_fusion.5
  337.2 2.0 multiply_reduce_fusion.5
  347.2 2.0 multiply_reduce_fusion.5
  357.2 2.0 multiply_reduce_fusion.5
  367.2 2.0 multiply_reduce_fusion.5
  369.3 1.9 fusion.151
  377.2 2.0 multiply_reduce_fusion.5
  381.2 1.9 fusion.152
  387.2 2.0 multiply_reduce_fusion.5
  391.2 1.9 fusion.152
  397.2 1.9 multiply_reduce_fusion.5
  399.3 1.9 fusion.151
  407.2 1.9 multiply_reduce_fusion.5
  409.3 1.9 fusion.151
  417.2 2.0 multiply_reduce_fusion.5
  427.2 2.0 multiply_reduce_fusion.5
  437.2 1.9 multiply_reduce_fusion.5
  439.3 1.9 fusion.151
  447.2 2.0 multiply_reduce_fusion.5
  457.1 1.9 multiply_reduce_fusion.5
  467.1 2.0 multiply_reduce_fusion.5
  477.1 2.0 multiply_reduce_fusion.5
  479.2 1.9 fusion.151
  486.3 2.2 collective-permute-start.2
  494.7 9.5 fusion.73
  504.3 10.7 %fusion.92 = f32[1024,4096]{1,0:T(8,128)} fusion(bf16[384,4096]{1,0:T(8,128)(2,1)} %copy-done.11, f32[384,1024]{1,0:T(8,128)S(1)} %get-tuple-element.305, f32[1024]{0:T(1024)S(1)} %convert_element_type.145, f32[1024]{0:T(1024)S(1)} %convert_element_type.144, f32[384]{0:T(512)S(1)} %fusion.85, f32[384]{0:T(512)S(1)} %broadcast_multiply_fusion), kind=kOutput, calls=%fused_computation.149 | convolution fusion | flops 3223191552 | bytes 21507072 | tf_op jit(solution)/shard_map/dot_general | solution.py:33
  516.1 10.9 %fusion.76 = f32[4096,1024]{1,0:T(8,128)} fusion(bf16[384,4096]{1,0:T(8,128)(2,1)} %get-tuple-element.294, bf16[1,384,1024]{2,1,0:T(8,128)(2,1)S(1)} %copy-done.4), kind=kOutput, calls=%fused_computation.127 | convolution fusion | flops 3221225472 | bytes 20709376 | tf_op jit(solution)/shard_map/dot_general | solution.py:33
  528.6 9.4 fusion.71
  538.0 6.0 fusion.93
  547.2 43.5 %all-reduce.18 = (f32[1024]{0:T(1024)S(1)}, f32[1024]{0:T(1024)S(1)}, f32[1024]{0:T(1024)S(1)}, f32[1024]{0:T(1024)S(1)}, f32[1024]{0:T(1024)S(1)}, /*index=5*/f...) all-reduce(f32[1024]{0:T(1024)S(1)} %get-tuple-element.204, ...), channel_id=2, replica_groups=mesh['dp'=16,'role'=2] {'dp','role'}, use_global_device_ids=true, to_apply=%region_16.17.clone | all-reduce | flops 12288 | bytes 98304
  595.9 61.7 %reduce-scatter.5.cloned.1.call-done = f32[32,3072]{1,0:T(8,128)} async-done(((f32[1024,3072]{1,0:T(8,128)}), f32[32,3072]{1,0:T(8,128)}) %reduce-scatter.5.cloned.1.call-update) | async-done | bytes 393232 | tf_op jit(solution)/shard_map/reduce_scatter | solution.py:224
  657.6 186.6 %reduce-scatter.9.cloned.1.call-done = f32[32,4096]{1,0:T(8,128)} async-done(((f32[1024,4096]{1,0:T(8,128)}), f32[32,4096]{1,0:T(8,128)}) %reduce-scatter.9.cloned.1.call-update) | async-done | bytes 524304 | tf_op jit(solution)/shard_map/reduce_scatter | solution.py:231
  844.3 187.5 %reduce-scatter.11.cloned.1.call-done = f32[128,1024]{1,0:T(8,128)} async-done(((f32[4096,1024]{1,0:T(8,128)}), f32[128,1024]{1,0:T(8,128)}) %reduce-scatter.11.cloned.1.call-update) | async-done | bytes 524304 | tf_op jit(solution)/shard_map/reduce_scatter | solution.py:233
  (356 shorter events, 211.3 us)
Async XLA Ops:
  7.2 51.5 %copy-start = (bf16[1,384,1024]{2,1,0:T(8,128)(2,1)S(1)}, bf16[1,384,1024]{2,1,0:T(8,128)(2,1)}, u32[]{:S(2)}) copy-start(bf16[1,384,1024]{2,1,0:T(8,128)(2,1)} %param.22) | copy-start | bytes 2359300
  7.2 75.8 %all-gather.6.cloned.1.call-start = ((), (), s32[]{:S(2)}) async-start(), calls=%async_computation.4 | async-start | bytes 6488064 | tf_op jit(solution)/shard_map/all_gather | solution.py:67
  7.9 211.2 %all-gather.8.cloned.1.call-start = ((), (), s32[]{:S(2)}) async-start(), calls=%async_computation.5 | async-start | bytes 2162688 | tf_op jit(solution)/shard_map/all_gather | solution.py:70
  8.7 213.5 %all-gather.10.cloned.1.call-start = ((), (), s32[]{:S(2)}) async-start(), calls=%async_computation.6 | async-start | bytes 8650752 | tf_op jit(solution)/shard_map/all_gather | solution.py:134
  9.4 289.5 %all-gather.12.cloned.1.call-start = ((), (), s32[]{:S(2)}) async-start(), calls=%async_computation.7 | async-start | bytes 8650752 | tf_op jit(solution)/shard_map/all_gather | solution.py:136
  59.0 29.0 %copy-start.16 = (f32[384]{0:T(512)}, f32[384]{0:T(512)S(1)}, u32[]{:S(2)}) copy-start(f32[384]{0:T(512)S(1)} %fusion.64) | copy-start | bytes 4612
  89.3 2.9 copy-start.18
  89.3 4.3 copy-start.19
  89.3 45.3 %collective-permute-start.1 = (bf16[384,1024]{1,0:T(8,128)(2,1)S(1)}, bf16[384,1024]{1,0:T(8,128)(2,1)S(1)}, u32[]{:S(2)}, u32[]{:S(2)}) collective-permute-start(bf16[384,1024]{1,0:T(8,128)(2,1)S(1)} %get-tuple-element.300), channel_id=1, source_target_pairs={{0,1},{2,3},{4,5},{6,7},{8,9},{10,11},{12,13},{14,15},{16,17},{18,... | collective-permute-start | bytes 2359304 | tf_op jit(solution)/shard_map/ppermute | solution.py:18
  90.8 45.1 %collective-permute-start = (bf16[384,1024]{1,0:T(8,128)(2,1)S(1)}, bf16[384,1024]{1,0:T(8,128)(2,1)}, u32[]{:S(2)}, u32[]{:S(2)}) collective-permute-start(bf16[384,1024]{1,0:T(8,128)(2,1)S(1)} %slice.59), channel_id=1, source_target_pairs={{0,1},{2,3},{4,5},{6,7},{8,9},{10,11},{12,13},{14,15},{16,17},{18,... | collective-permute-start | bytes 2359304 | tf_op jit(solution)/shard_map/ppermute | solution.py:18
  92.1 503.8 %reduce-scatter.7.cloned.1.call-start = ((), (), s32[]{:S(2)}) async-start(), calls=%async_computation.9 | async-start | bytes 4325376 | tf_op jit(solution)/shard_map/reduce_scatter | solution.py:227
  298.9 11.1 %copy-start.20 = (bf16[1024,4096]{1,0:T(8,128)(2,1)S(1)}, bf16[1024,4096]{1,0:T(8,128)(2,1)}, u32[]{:S(2)}) copy-start(bf16[1024,4096]{1,0:T(8,128)(2,1)} %all-gather.10.cloned.1.call-done) | copy-start | bytes 25165828
  309.9 3.9 copy-start.11
  313.8 1.1 copy-start.3
  314.4 1.2 copy-start.1
  315.6 0.9 copy-start.12
  319.8 1.1 copy-start.13
  319.9 337.8 %reduce-scatter.5.cloned.1.call-start = ((), (), s32[]{:S(2)}) async-start(), calls=%async_computation.8 | async-start | bytes 12976128 | tf_op jit(solution)/shard_map/reduce_scatter | solution.py:224
  484.4 9.4 copy-start.5
  484.4 7.3 copy-start.14
  486.3 5.7 collective-permute-start.2
  490.0 1.9 copy-start.15
  490.0 3.5 collective-permute-start.3
  492.2 1.6 copy-start.7
  493.8 0.9 copy-start.9
  504.2 340.1 %reduce-scatter.9.cloned.1.call-start = ((), (), s32[]{:S(2)}) async-start(), calls=%async_computation.10 | async-start | bytes 17301504 | tf_op jit(solution)/shard_map/reduce_scatter | solution.py:231
  514.9 1.2 copy-start.4
  515.0 516.8 %reduce-scatter.11.cloned.1.call-start = ((), (), s32[]{:S(2)}) async-start(), calls=%async_computation.11 | async-start | bytes 17301504 | tf_op jit(solution)/shard_map/reduce_scatter | solution.py:233
  528.6 9.4 copy-start.6
  528.6 9.4 copy-start.8
  528.6 9.4 copy-start.10
  538.0 6.0 copy-start.17
  544.0 1.5 copy-start.2
Sparse Core Ops, SparseCore 0:
  10.9 72.0 all-gather.5
  85.9 54.9 all-gather.7
  143.8 76.2 all-gather.9
  222.8 76.0 all-gather.11
  320.0 133.9 reduce-scatter.6
  504.3 153.2 reduce-scatter.4
  660.6 183.6 reduce-scatter.8
  847.2 184.4 reduce-scatter.10
where the time goes:
time: 1050 us; the launch traced here: 1040 us
  waiting for transfers between devices  520 us (50%)
  matrix products  286 us (27%)
  blocking collectives  126 us (12%)
  local copies, waits for them, and re-layouts  41.6 us (4%)
  loops' own time  22.1 us (2%)
  other arithmetic  20.8 us (2%)
  between operations  16.2 us (2%)
    reduce_scatter x1, waiting for transfers between devices, shards(): lax.psum_scatter(reduce_weight_term, ('dp', 'role'), scatter_dimension=0,...  187 us
    reduce_scatter x1, waiting for transfers between devices, shards(): lax.psum_scatter(expand_weight_term, ('dp', 'role'), scatter_dimension=0,...  187 us
    dot_general x52, matrix products, outer_cols(): lax.dot_general(left, right, (((1,), (1,)), ((), ())), preferred_element_...  107 us
    dot_general x36, matrix products, inner_rows(): lax.dot_general(left, right, (((0,), (0,)), ((), ())), preferred_element_...  95.4 us
    unnamed x2, blocking collectives  84.6 us
    reduce_scatter x1, waiting for transfers between devices, shards(): lax.psum_scatter(inward_weight_term, ('dp', 'role'), scatter_dimension=0,...  61.7 us
    all_gather x1, waiting for transfers between devices, shards(): lax.all_gather(reduce_weight, ('dp', 'role'), axis=0, tiled=True)  56.2 us
    all_gather x1, blocking collectives, shards(): lax.all_gather(expand_bias, ('dp', 'role'), axis=0, tiled=True)  40.9 us
  transfers between devices with their start and end apart: 12, of which 6 were waited for; matrix products, arithmetic and copies ran while one was open for 31% of the time, Pallas kernels for 0%

commit v1 on v0

--- a/solution.py
+++ b/solution.py
@@ -1,15 +1,948 @@
+import functools
+
 import jax
 import jax.numpy as jnp
 from jax import lax
+from jax.experimental import pallas as pl
+from jax.experimental.pallas import tpu as pltpu
 from jax.sharding import PartitionSpec as P
 
 D = 1024
 H = 16
 HD = 64
-
-
 EPS = 1e-05
 MASKED = -1e30
+LOG2E = 1.4426950408889634
+BF = jnp.bfloat16
+F32 = jnp.float32
+MESH = pl.DeviceIdType.MESH
+
+
+def dot(left, right):
+    return lax.dot_general(left, right, (((1,), (0,)), ((), ())), preferred_element_type=F32)
+
+
+def dot_nt(left, right):
+    return lax.dot_general(left, right, (((1,), (1,)), ((), ())), preferred_element_type=F32)
+
+
+def flip(value):
+    return value.astype(F32).T.astype(value.dtype)
+
+
+def centre(values):
+    mean_value = jnp.mean(values, axis=-1, keepdims=True)
+    centered = values - mean_value
+    spread = jnp.mean(centered * centered, axis=-1, keepdims=True)
+    return centered * lax.rsqrt(spread + EPS), lax.rsqrt(spread + EPS)
+
+
+def norm_back(unit, rate, gain, upstream):
+    pulled = upstream * gain
+    first = jnp.mean(pulled, axis=-1, keepdims=True)
+    second = jnp.mean(pulled * unit, axis=-1, keepdims=True)
+    return rate * (pulled - first - unit * second)
+
+
+SLOTS = 3
+
+
+def scratch_list():
+    dma = pltpu.SemaphoreType.DMA
+    v = pltpu.VMEM
+    return dict(
+        small=v((4, 2, 2, 2, 16, 128), BF),
+        vec=v((8, 1024), F32),
+        ebias=v((4, 8, 512), F32),
+        frames_all=v((2, 384, 1024), BF),
+        c_all=v((2, 384, 1024), BF),
+        n_all=v((2, 384, 1024), BF),
+        n1t=v((1024, 768), BF),
+        n2t=v((1024, 768), BF),
+        win=v((3, 4, 2, 2, 64, 512), BF),
+        wout=v((4, 2, 2, 2, 32, 1024), BF),
+        wexp=v((4, 4, 2, 2, 64, 512), BF),
+        wred=v((4, 2, 2, 128, 1024), BF),
+        stage=v((2, 32, 2048), BF),
+        qkv=v((3, 4, 768, 128), BF),
+        mask=v((768, 768), BF),
+        lse=v((4, 6, 8, 256), F32),
+        half=v((2, 384, 512), BF),
+        half_t=v((2, 512, 384), BF),
+        wide=v((384, 1024), BF),
+        att_t=v((1024, 384), BF),
+        middle=v((384, 1024), F32),
+        out_acc=v((2, 384, 1024), F32),
+        bn_acc=v((2, 384, 1024), F32),
+        cross=v((2, 384, 1024), F32),
+        ffb=v((3, 768, 512), BF),
+        act_t=v((512, 768), BF),
+        ba_all=v((2, 384, 512), BF),
+        dkv=v((2, 768, 128), F32),
+        gvec=v((8, 1024), F32),
+        gexp=v((4, 8, 512), F32),
+        outx=v((4, 2, 2, 32, 1024), BF),
+        rb=v((SLOTS, 2, 4, 64, 512), BF),
+        ra=v((SLOTS, 4, 64, 512), BF),
+        rz=v((7, 3, 64, 512), BF),
+        rb_red=v((SLOTS, 2, 128, 1024), BF),
+        ra_red=v((SLOTS, 128, 1024), BF),
+        rz_red=v((3, 128, 1024), BF),
+        rb_out=v((2, 4, 32, 1024), BF),
+        ra_out=v((4, 32, 1024), BF),
+        rz_out=v((3, 32, 1024), BF),
+        sg=v((4, 2, 2, 16, 128), F32),
+        rb_sg=v((2, 4, 16, 128), F32),
+        ra_sg=v((4, 16, 128), F32),
+        rz_sg=v((3, 16, 128), F32),
+        fin=v((7, 64, 512), F32),
+        fin_in=v((7, 32, 512), F32),
+        sfin=v((16, 128), F32),
+        sfin_in=v((16, 128), F32),
+        own_s=dma((2,)),
+        pre_s=dma((10,)),
+        pre_r=dma((10,)),
+        agz_s=dma((13, 3)),
+        agz_r=dma((13, 3)),
+        aga_s=dma((13,)),
+        aga_r=dma((13,)),
+        agb_s=dma((13, 2)),
+        agb_r=dma((13, 2)),
+        core_s=dma((9,)),
+        core_r=dma((9,)),
+        rsb_s=dma((13, 2)),
+        rsb_r=dma((13, 2)),
+        rsa_s=dma((13,)),
+        rsa_r=dma((13,)),
+        rsz_s=dma((13, 3)),
+        rsz_r=dma((13, 3)),
+        fin_s=dma((8,)),
+        fin_r=dma((8,)),
+    )
+
+
+class Bag:
+    def __init__(self, **kw):
+        self.__dict__.update(kw)
+
+
+N_IN = 10
+N_OUT = 7
+
+
+def layer_kernel(names, *refs):
+    (phon_ref, prom_ref, seg_ref, frames_ref, cot_ref, small_in, win_in, wout_in, wexp_in, wred_in) = refs[:N_IN]
+    (result_ref, fgrad_ref, dwin_ref, dwout_ref, dwexp_ref, dwred_ref, dsmall_ref) = refs[N_IN : N_IN + N_OUT]
+    s = Bag(**dict(zip(names, refs[N_IN + N_OUT :])))
+
+    dp = lax.axis_index("dp")
+    r = lax.axis_index("role")
+    o = 1 - r
+    z, y, x = dp // 4, (dp // 2) % 2, dp % 2
+    ya, xa = y + r * (1 - 2 * y), x + (1 - r) * (1 - 2 * x)
+    yb, xb = y + (1 - r) * (1 - 2 * y), x + r * (1 - 2 * x)
+    yc, xc = 1 - y, 1 - x
+    core_dev = (dp, o)
+    a_dev = (z * 4 + ya * 2 + xa, r)
+    b_dev = (z * 4 + yb * 2 + xb, r)
+    z_dev = [(((z + k) % 4) * 4 + y * 2 + x, r) for k in (1, 2, 3)]
+    z_at = [(z + k) % 4 for k in (1, 2, 3)]
+    z_from = [(z + 4 - k) % 4 for k in (1, 2, 3)]
+
+    def copy(src, dst, ss, rs, dev):
+        return pltpu.make_async_remote_copy(
+            src_ref=src, dst_ref=dst, send_sem=ss, recv_sem=rs, device_id=dev, device_id_type=MESH
+        )
+
+    barrier = pltpu.get_barrier_semaphore()
+    for dev in z_dev + [a_dev, b_dev, core_dev]:
+        pl.semaphore_signal(barrier, inc=1, device_id=dev, device_id_type=MESH)
+    pl.semaphore_wait(barrier, 6)
+
+    my_rows = pl.ds(pl.multiple_of(r * 32, 32), 32)
+    o_rows = pl.ds(pl.multiple_of(o * 32, 32), 32)
+
+    def half_cols(section, who):
+        return pl.ds(pl.multiple_of(section * 1024 + who * 512, 512), 512)
+
+    for block in range(16):
+        for who in range(2):
+            s.stage[who, :, block * 128 : (block + 1) * 128] = wexp_in[
+                :, (2 * block + who) * 128 : (2 * block + who + 1) * 128
+            ]
+    pre = []
+    pre.append(copy(small_in, s.small.at[z, y, x, r], s.pre_s.at[0], s.pre_r.at[0], core_dev))
+    for i in range(3):
+        pre.append(
+            copy(
+                win_in.at[:, half_cols(i, o)],
+                s.win.at[i, z, y, x, my_rows],
+                s.pre_s.at[1 + i],
+                s.pre_r.at[1 + i],
+                core_dev,
+            )
+        )
+    pre.append(copy(frames_ref, s.frames_all.at[r], s.pre_s.at[4], s.pre_r.at[4], core_dev))
+    for j in range(4):
+        pre.append(
+            copy(
+                s.stage.at[o, :, pl.ds(j * 512, 512)],
+                s.wexp.at[j, z, y, x, my_rows],
+                s.pre_s.at[5 + j],
+                s.pre_r.at[5 + j],
+                core_dev,
+            )
+        )
+    pre.append(copy(cot_ref, s.c_all.at[r], s.pre_s.at[9], s.pre_r.at[9], core_dev))
+    for item in pre:
+        item.start()
+    own_frames = pltpu.make_async_copy(frames_ref, s.frames_all.at[r], s.own_s.at[0])
+    own_cot = pltpu.make_async_copy(cot_ref, s.c_all.at[r], s.own_s.at[1])
+    own_frames.start()
+    own_cot.start()
+    s.small[z, y, x, r] = small_in[...]
+    for i in range(3):
+        s.win[i, z, y, x, my_rows] = win_in[:, half_cols(i, r)]
+    s.wout[z, y, x, r] = wout_in[...]
+    s.wred[z, y, x] = wred_in[...]
+    for j in range(4):
+        s.wexp[j, z, y, x, my_rows] = s.stage[r, :, j * 512 : (j + 1) * 512]
+
+    def ag_small():
+        return Bag(t=0, piece=lambda a, b, c: s.small.at[a, b, c], col=lambda b, c: s.small.at[:, b, c], plane=None)
+
+    def ag_in(i):
+        return Bag(
+            t=1 + i, piece=lambda a, b, c: s.win.at[i, a, b, c], col=lambda b, c: s.win.at[i, :, b, c], plane=None
+        )
+
+    def ag_out():
+        return Bag(
+            t=4, piece=lambda a, b, c: s.wout.at[a, b, c, r], col=lambda b, c: s.wout.at[:, b, c, r], plane=None
+        )
+
+    def ag_exp(j):
+        return Bag(
+            t=5 + 2 * j,
+            piece=lambda a, b, c: s.wexp.at[j, a, b, c],
+            col=lambda b, c: s.wexp.at[j, :, b, c],
+            plane=None,
+        )
+
+    def ag_red(j):
+        return Bag(
+            t=6 + 2 * j, piece=lambda a, b, c: s.wred.at[j, b, c], col=lambda b, c: s.wred.at[j, b, c], plane=j
+        )
+
+    def z_copies(it):
+        return [
+            copy(it.piece(z, y, x), it.piece(z, y, x), s.agz_s.at[it.t, k], s.agz_r.at[it.t, k], z_dev[k])
+            for k in range(3)
+        ]
+
+    def a_copy(it, yy, xx):
+        return copy(it.col(yy, xx), it.col(yy, xx), s.aga_s.at[it.t], s.aga_r.at[it.t], a_dev)
+
+    def b_copy(it, which, yy, xx):
+        return copy(it.col(yy, xx), it.col(yy, xx), s.agb_s.at[it.t, which], s.agb_r.at[it.t, which], b_dev)
+
+    def e0(it):
+        def go():
+            for c in z_copies(it):
+                c.start()
+
+        if it.plane is None:
+            go()
+        else:
+            pl.when(z == it.plane)(go)
+
+    def e1(it):
+        if it.plane is None:
+            for k in range(3):
+                p = it.piece(z_from[k], y, x)
+                copy(p, p, s.agz_s.at[it.t, k], s.agz_r.at[it.t, k], z_dev[k]).wait_recv()
+        else:
+
+            @pl.when(z != it.plane)
+            def _():
+                k = (z + 4 - it.plane) % 4 - 1
+                p = it.piece(z, y, x)
+                copy(p, p, s.agz_s.at[it.t, k], s.agz_r.at[it.t, k], z_dev[0]).wait_recv()
+
+        a_copy(it, y, x).start()
+        b_copy(it, 0, y, x).start()
+
+    def e2(it):
+        a_copy(it, ya, xa).wait_recv()
+        b_copy(it, 1, ya, xa).start()
+
+    def e3(it):
+        b_copy(it, 0, yb, xb).wait_recv()
+        b_copy(it, 1, yc, xc).wait_recv()
+
+    def sent(it):
+        def go():
+            for c in z_copies(it):
+                c.wait_send()
+
+        if it.plane is None:
+            go()
+        else:
+            pl.when(z == it.plane)(go)
+        a_copy(it, y, x).wait_send()
+        b_copy(it, 0, y, x).wait_send()
+        b_copy(it, 1, ya, xa).wait_send()
+
+    i_small, i_q, i_k, i_v, i_out = ag_small(), ag_in(0), ag_in(1), ag_in(2), ag_out()
+
+    def pre_in(index, dst):
+        copy(dst, dst, s.pre_s.at[index], s.pre_r.at[index], core_dev).wait_recv()
+
+    pre_in(0, s.small.at[z, y, x, o])
+    e0(i_small)
+    pre_in(1, s.win.at[0, z, y, x, o_rows])
+    e0(i_q)
+    e1(i_small)
+    pre_in(2, s.win.at[1, z, y, x, o_rows])
+    e0(i_k)
+
+    own_frames.wait()
+    own_cot.wait()
+    prefix = phon_ref[0] + prom_ref[0]
+    seg_row = seg_ref[...].astype(F32)
+    seg_wide = jnp.broadcast_to(seg_row, (384, 384))
+    seg_tall = seg_wide.T
+    key_at = lax.broadcasted_iota(jnp.int32, (384, 384), 0)
+    row_at = lax.broadcasted_iota(jnp.int32, (384, 384), 1)
+    causal = key_at <= row_at
+    seen = key_at < prefix
+
+    def as_bias(allowed):
+        return jnp.where(allowed, 0.0, MASKED).astype(BF)
+
+    s.mask[0:384, 0:384] = as_bias(causal & seen)
+    s.mask[0:384, 384:768] = as_bias(seen)
+    s.mask[384:768, 384:768] = as_bias(causal & (seg_wide == seg_tall))
+
+    e1(i_q)
+    e2(i_small)
+    pre_in(3, s.win.at[2, z, y, x, o_rows])
+    e0(i_v)
+    e1(i_k)
+    e2(i_q)
+    e3(i_small)
+
+    def tile_sum(q):
+        total = jnp.zeros((16, 128), F32)
+        for xx in range(2):
+            for who in range(2):
+                total = total + s.small[q // 2, q % 2, xx, who].astype(F32)
+        return total
+
+    for q in range(8):
+        s.vec[:, q * 128 : (q + 1) * 128] = tile_sum(q)[0:8]
+    for j in range(4):
+        for yy in range(2):
+            for xx in range(2):
+                at = (yy * 2 + xx) * 128
+                s.ebias[j, 0:1, at : at + 128] = s.small[j, yy, xx, r].astype(F32)[8:9]
+
+    def vec_row(i):
+        return s.vec[i : i + 1, :]
+
+    pre_in(4, s.frames_all.at[o])
+
+    def norm_tile(i, carry):
+        who, rows = i // 3, pl.ds(pl.multiple_of((i % 3) * 128, 128), 128)
+        unit, _ = centre(s.frames_all[who, rows].astype(F32))
+        normed = unit * vec_row(0) + vec_row(1)
+        s.n_all[who, rows] = normed.astype(BF)
+        s.n1t[:, pl.ds(pl.multiple_of(i * 128, 128), 128)] = normed.T.astype(BF)
+        return carry
+
+    lax.fori_loop(0, 6, norm_tile, 0)
+
+    def project(i):
+        def body(n, carry):
+            cols = pl.ds(pl.multiple_of(n * 256, 256), 256)
+            weight = s.win[i, :, :, :, :, cols].reshape(1024, 256)
+            left = s.n_all[...].reshape(768, 1024)
+            mixed = dot(left, weight)
+            if i != 1:
+                bias_at = pl.ds(pl.multiple_of(r * 512 + n * 256, 256), 256)
+                bias_row = 2 if i == 0 else 3
+                mixed = mixed + s.vec[bias_row : bias_row + 1, bias_at]
+            mixed = mixed.astype(BF)
+            s.qkv[i, 2 * n] = mixed[:, 0:128]
+            s.qkv[i, 2 * n + 1] = mixed[:, 128:256]
+            return carry
+
+        lax.fori_loop(0, 2, body, 0)
+
+    e0(i_out)
+    e1(i_v)
+    e2(i_k)
+    e3(i_q)
+    project(0)
+    for j in range(4):
+        pre_in(5 + j, s.wexp.at[j, z, y, x, o_rows])
+    e0(ag_exp(0))
+    e1(i_out)
+    e2(i_v)
+    e3(i_k)
+    project(1)
+    e0(ag_red(0))
+    e1(ag_exp(0))
+    e2(i_out)
+    e3(i_v)
+    project(2)
+
+    factor = HD**-0.5 * LOG2E
+    low_lane = lax.broadcasted_iota(jnp.int32, (128, 128), 1) < 64
+
+    def pair_rows(block):
+        zero = jnp.zeros_like(block)
+        return jnp.concatenate([jnp.where(low_lane, block, zero), jnp.where(low_lane, zero, block)], axis=0)
+
+    def pair_mask(keys, rb):
+        bias = s.mask[0:keys, rb * 128 : (rb + 1) * 128].astype(F32)
+        return jnp.concatenate([bias, bias], axis=1)
+
+    def key_count(rb):
+        return (rb + 1) * 128 if rb < 3 else 384 + (rb - 2) * 128
+
+    def attend(hp, carry):
+        v_t = flip(s.qkv[2, hp])
+        dims = pl.ds(pl.multiple_of(hp * 128, 128), 128)
+        for rb in range(6):
+            keys = key_count(rb)
+            both = pair_rows(s.qkv[0, hp, rb * 128 : (rb + 1) * 128])
+            scores = dot_nt(s.qkv[1, hp, 0:keys], both) * factor + pair_mask(keys, rb)
+            peak = jnp.max(scores, axis=0, keepdims=True)
+            expo = jnp.exp2(scores - peak)
+            total = jnp.sum(expo, axis=0, keepdims=True)
+            heads = dot(v_t[:, 0:keys], expo.astype(BF)) / total
+            s.lse[hp, rb] = jnp.broadcast_to(peak + jnp.log2(total), (8, 256))
+            out = jnp.concatenate([heads[0:64, 0:128], heads[64:128, 128:256]], axis=0)
+            at = (rb % 3) * 128
+            s.half_t[rb // 3, dims, at : at + 128] = out.astype(BF)
+            s.half[rb // 3, at : at + 128, dims] = out.T.astype(BF)
+        return carry
+
+    lax.fori_loop(0, 4, attend, 0)
+
+    my_half = pl.ds(pl.multiple_of(r * 512, 512), 512)
+    o_half = pl.ds(pl.multiple_of(o * 512, 512), 512)
+
+    def core_copy(index, src, dst):
+        return copy(src, dst, s.core_s.at[index], s.core_r.at[index], core_dev)
+
+    core_copy(0, s.half.at[o], s.wide.at[:, my_half]).start()
+    core_copy(1, s.half_t.at[o], s.att_t.at[my_half]).start()
+    s.wide[:, my_half] = s.half[r]
+    s.att_t[my_half] = s.half_t[r]
+    e0(ag_exp(1))
+    e1(ag_red(0))
+    e2(ag_exp(0))
+    e3(i_out)
+    out_swap = core_copy(2, s.wout.at[:, :, :, r], s.wout.at[:, :, :, r])
+    out_swap.start()
+    core_copy(0, s.wide.at[:, o_half], s.wide.at[:, o_half]).wait_recv()
+    core_copy(1, s.att_t.at[o_half], s.att_t.at[o_half]).wait_recv()
+    core_copy(2, s.wout.at[:, :, :, o], s.wout.at[:, :, :, o]).wait_recv()
+
+    def out_tile(n, carry):
+        cols = pl.ds(pl.multiple_of(n * 256, 256), 256)
+        branch = dot(s.wide[...], s.wout[:, :, :, :, :, cols].reshape(1024, 256))
+        s.middle[:, cols] = s.frames_all[r, :, cols].astype(F32) + branch + s.vec[4:5, cols]
+        return carry
+
+    lax.fori_loop(0, 4, out_tile, 0)
+
+    def norm_two(i, carry):
+        rows = pl.ds(pl.multiple_of(i * 128, 128), 128)
+        unit, _ = centre(s.middle[rows])
+        s.n_all[r, rows] = (unit * vec_row(5) + vec_row(6)).astype(BF)
+        return carry
+
+    lax.fori_loop(0, 3, norm_two, 0)
+    core_copy(3, s.n_all.at[r], s.n_all.at[r]).start()
+    pre_in(9, s.c_all.at[o])
+    s.out_acc[...] = jnp.zeros_like(s.out_acc)
+    s.bn_acc[...] = jnp.zeros_like(s.bn_acc)
+    core_copy(3, s.n_all.at[o], s.n_all.at[o]).wait_recv()
+
+    def flip_two(i, carry):
+        who, rows = i // 3, pl.ds(pl.multiple_of((i % 3) * 128, 128), 128)
+        s.n2t[:, pl.ds(pl.multiple_of(i * 128, 128), 128)] = flip(s.n_all[who, rows])
+        return carry
+
+    lax.fori_loop(0, 6, flip_two, 0)
+
+    def feed(j, carry):
+        more = j < 3
+
+        @pl.when(more)
+        def _():
+            e0(ag_red(j + 1))
+            e1(ag_exp(j + 1))
+
+        e2(ag_red(j))
+        e3(ag_exp(j))
+
+        @pl.when(j < 2)
+        def _():
+            e0(ag_exp(j + 2))
+
+        @pl.when(more)
+        def _():
+            e1(ag_red(j + 1))
+            e2(ag_exp(j + 1))
+
+        e3(ag_red(j))
+        sent(ag_exp(j))
+        sent(ag_red(j))
+
+        def hidden(n, inside):
+            cols = pl.ds(pl.multiple_of(n * 256, 256), 256)
+            left = s.n_all[...].reshape(768, 1024)
+            inner = dot(left, s.wexp[j, :, :, :, :, cols].reshape(1024, 256)) + s.ebias[j, 0:1, cols]
+            phi = 0.5 + 0.5 * lax.erf(inner * (2.0**-0.5))
+            active = inner * phi
+            s.ffb[0, :, cols] = active.astype(BF)
+            s.act_t[cols] = active.T.astype(BF)
+            slope = phi + inner * (jnp.exp(-0.5 * inner * inner) * 0.3989422804014327)
+            up = s.c_all[...].reshape(768, 1024)
+            back = (dot_nt(up, s.wred[j, n].reshape(256, 1024)) * slope).astype(BF)
+            s.ffb[1, :, cols] = back
+            s.gexp[j, 0:1, cols] = jnp.sum(back.astype(F32), axis=0, keepdims=True)
+            return inside
+
+        lax.fori_loop(0, 2, hidden, 0)
+
+        def wide_tile(n, inside):
+            cols = pl.ds(pl.multiple_of(n * 256, 256), 256)
+            part = dot(s.ffb[0], s.wred[j, :, :, :, cols].reshape(512, 256))
+            s.out_acc[:, :, cols] += part.reshape(2, 384, 256)
+            back = dot_nt(s.ffb[1], s.wexp[j, n].reshape(256, 512))
+            s.bn_acc[:, :, cols] += back.reshape(2, 384, 256)
+            return inside
+
+        lax.fori_loop(0, 4, wide_tile, 0)
+
+        def grad_red(n, inside):
+            cols = pl.ds(pl.multiple_of(n * 256, 256), 256)
+            up = s.c_all[:, :, cols].reshape(768, 256)
+            s.wred[j, :, :, :, cols] = dot(s.act_t[...], up).astype(BF).reshape(2, 2, 128, 256)
+            return inside
+
+        lax.fori_loop(0, 4, grad_red, 0)
+
+        def grad_exp(n, inside):
+            cols = pl.ds(pl.multiple_of(n * 256, 256), 256)
+            grad = dot(s.n2t[...], s.ffb[1, :, cols]).astype(BF)
+            s.wexp[j, :, :, :, :, cols] = grad.reshape(4, 2, 2, 64, 256)
+            return inside
+
+        lax.fori_loop(0, 2, grad_exp, 0)
+        return carry
+
+    lax.fori_loop(0, 4, feed, 0)
+
+    def rs_exp(j):
+        return Bag(
+            t=j, fin=j, parts=4, plane=None, piece=lambda a, b, c: s.wexp.at[j, a, b, c],
+            col=lambda b, c: s.wexp.at[j, :, b, c], rb=lambda w: s.rb.at[j % SLOTS, w], ra=s.ra.at[j % SLOTS],
+            rz=lambda k: s.rz.at[j, k],
+        )
+
+    def rs_in(i):
+        return Bag(
+            t=9 + i, fin=4 + i, parts=4, plane=None, piece=lambda a, b, c: s.win.at[i, a, b, c],
+            col=lambda b, c: s.win.at[i, :, b, c], rb=lambda w: s.rb.at[(4 + i) % SLOTS, w],
+            ra=s.ra.at[(4 + i) % SLOTS], rz=lambda k: s.rz.at[4 + i, k],
+        )
+
+    def rs_red(j):
+        return Bag(
+            t=4 + j, fin=None, parts=1, plane=j, piece=lambda a, b, c: s.wred.at[j, b, c],
+            col=lambda b, c: s.wred.at[j, b, c], rb=lambda w: s.rb_red.at[j % SLOTS, w],
+            ra=s.ra_red.at[j % SLOTS], rz=lambda k: s.rz_red.at[k],
+        )
+
+    def rs_out():
+        return Bag(
+            t=8, fin=None, parts=4, plane=None, piece=lambda a, b, c: s.wout.at[a, b, c, r],
+            col=lambda b, c: s.wout.at[:, b, c, r], rb=lambda w: s.rb_out.at[w], ra=s.ra_out,
+            rz=lambda k: s.rz_out.at[k],
+        )
+
+    def rs_small():
+        return Bag(
+            t=12, fin=None, parts=4, plane=None, piece=lambda a, b, c: s.sg.at[a, b, c],
+            col=lambda b, c: s.sg.at[:, b, c], rb=lambda w: s.rb_sg.at[w], ra=s.ra_sg,
+            rz=lambda k: s.rz_sg.at[k],
+        )
+
+    def rb_copy(it, which, yy, xx):
+        return copy(it.col(yy, xx), it.rb(which), s.rsb_s.at[it.t, which], s.rsb_r.at[it.t, which], b_dev)
+
+    def ra_copy(it):
+        return copy(it.col(ya, xa), it.ra, s.rsa_s.at[it.t], s.rsa_r.at[it.t], a_dev)
+
+    def rz_copy(it, k, at):
+        return copy(it.piece(at, y, x), it.rz(k), s.rsz_s.at[it.t, k], s.rsz_r.at[it.t, k], z_dev[k])
+
+    def add_into(it, yy, xx, sources):
+        target = it.col(yy, xx)
+        kind = F32 if it.t == 12 else BF
+
+        def one(at):
+            total = target[at].astype(F32)
+            for src in sources:
+                total = total + src[at].astype(F32)
+            target[at] = total.astype(kind)
+
+        if it.parts == 4:
+
+            def body(i, carry):
+                one(i)
+                return carry
+        else:
+
+            def body(i, carry):
+                one(pl.ds(pl.multiple_of(i * 32, 32), 32))
+                return carry
+
+        lax.fori_loop(0, 4, body, 0)
+
+    def f0(it):
+        rb_copy(it, 0, yc, xc).start()
+        rb_copy(it, 1, yb, xb).start()
+
+    def f1(it):
+        rb_copy(it, 0, yc, xc).wait_recv()
+        add_into(it, ya, xa, [it.rb(0)])
+        ra_copy(it).start()
+
+    def f2(it):
+        rb_copy(it, 1, yb, xb).wait_recv()
+        ra_copy(it).wait_recv()
+        add_into(it, y, x, [it.rb(1), it.ra])
+
+        if it.plane is None:
+            for k in range(3):
+                rz_copy(it, k, z_at[k]).start()
+        else:
+
+            @pl.when(z != it.plane)
+            def _():
+                k = (it.plane + 4 - z) % 4 - 1
+                copy(
+                    it.piece(z, y, x), it.rz(k), s.rsz_s.at[it.t, k], s.rsz_r.at[it.t, k],
+                    (it.plane * 4 + y * 2 + x, r),
+                ).start()
+
+    def z_total(it):
+        for k in range(3):
+            rz_copy(it, k, z_at[k]).wait_recv()
+        total = it.piece(z, y, x)[...].astype(F32)
+        for k in range(3):
+            total = total + it.rz(k)[...].astype(F32)
+        return total
+
+    def fin_copy(index):
+        return copy(s.fin.at[index, o_rows], s.fin_in.at[index], s.fin_s.at[index], s.fin_r.at[index], core_dev)
+
+    def small_fin():
+        return copy(s.sfin, s.sfin_in, s.fin_s.at[7], s.fin_r.at[7], core_dev)
+
+    def put(index, value, who):
+        if index < 4:
+            for i in range(4):
+                at = pl.ds(pl.multiple_of((2 * (4 * index + i) + who) * 128, 128), 128)
+                dwexp_ref[:, at] = value[:, i * 128 : (i + 1) * 128]
+        else:
+            dwin_ref[:, half_cols(index - 4, who)] = value
+
+    def f4(it):
+        if it.plane is not None:
+
+            @pl.when(z == it.plane)
+            def _():
+                dwred_ref[...] = z_total(it)
+        elif it.t == 8:
+            dwout_ref[...] = z_total(it)
+        elif it.t == 12:
+            s.sfin[...] = z_total(it)
+            small_fin().start()
+        else:
+            s.fin[it.fin] = z_total(it)
+            fin_copy(it.fin).start()
+            put(it.fin, s.fin[it.fin, my_rows], r)
+
+    def f5(it):
+        if it.fin is not None:
+            fin_copy(it.fin).wait_recv()
+            put(it.fin, s.fin_in[it.fin], o)
+        elif it.t == 12:
+            small_fin().wait_recv()
+            row = lax.broadcasted_iota(jnp.int32, (16, 128), 0)
+            own = s.sfin[...]
+            dsmall_ref[...] = jnp.where(row < 8, own + s.sfin_in[...], own)
+
+    def all_sent(it):
+        rb_copy(it, 0, yc, xc).wait_send()
+        rb_copy(it, 1, yb, xb).wait_send()
+        ra_copy(it).wait_send()
+        if it.plane is None:
+            for k in range(3):
+                rz_copy(it, k, z_at[k]).wait_send()
+        else:
+
+            @pl.when(z != it.plane)
+            def _():
+                k = (it.plane + 4 - z) % 4 - 1
+                copy(
+                    it.piece(z, y, x), it.rz(k), s.rsz_s.at[it.t, k], s.rsz_r.at[it.t, k],
+                    (it.plane * 4 + y * 2 + x, r),
+                ).wait_send()
+        if it.fin is not None:
+            fin_copy(it.fin).wait_send()
+        elif it.t == 12:
+            small_fin().wait_send()
+
+    order = []
+    for j in range(4):
+        order += [rs_exp(j), rs_red(j)]
+    order += [rs_out(), rs_in(0), rs_in(1), rs_in(2), rs_small()]
+
+    def step(i):
+        for event, lag in ((f0, 0), (f1, 1), (f2, 2), (f4, 3), (f5, 4)):
+            if 0 <= i - lag < len(order):
+                event(order[i - lag])
+
+    core_copy(4, s.bn_acc.at[o], s.cross.at[0]).start()
+    core_copy(5, s.out_acc.at[o], s.cross.at[1]).start()
+    step(0)
+    core_copy(4, s.bn_acc.at[o], s.cross.at[0]).wait_recv()
+
+    def middle_back(i, carry):
+        rows = pl.ds(pl.multiple_of(i * 128, 128), 128)
+        unit, rate = centre(s.middle[rows])
+        upstream = s.bn_acc[r, rows] + s.cross[0, rows]
+        cot = s.c_all[r, rows].astype(F32)
+        back = cot + norm_back(unit, rate, vec_row(5), upstream)
+        s.bn_acc[r, rows] = back
+        branch = back.astype(BF)
+        s.wide[rows] = branch
+        gain_t, shift_t, out_t, red_t = carry
+        return (
+            gain_t + jnp.sum(upstream * unit, axis=0, keepdims=True),
+            shift_t + jnp.sum(upstream, axis=0, keepdims=True),
+            out_t + jnp.sum(branch.astype(F32), axis=0, keepdims=True),
+            red_t + jnp.sum(cot, axis=0, keepdims=True),
+        )
+
+    zero_row = jnp.zeros((1, 1024), F32)
+    gain_t, shift_t, out_t, red_t = lax.fori_loop(0, 3, middle_back, (zero_row,) * 4)
+    s.gvec[5:6] = gain_t
+    s.gvec[6:7] = shift_t
+    s.gvec[4:5] = out_t
+    s.gvec[7:8] = red_t
+
+    core_copy(0, s.half.at[o], s.half.at[o]).wait_send()
+    core_copy(2, s.wout.at[:, :, :, r], s.wout.at[:, :, :, r]).wait_send()
+
+    def back_att(n, carry):
+        weight = s.wout[n].reshape(256, 1024)
+        cols = pl.ds(pl.multiple_of((n % 2) * 256, 256), 256)
+        s.half[n // 2, :, cols] = dot_nt(s.wide[...], weight).astype(BF)
+        return carry
+
+    lax.fori_loop(0, 4, back_att, 0)
+    core_copy(6, s.half.at[o], s.ba_all.at[r]).start()
+    s.ba_all[r] = s.half[r]
+    step(1)
+    sent(i_out)
+
+    def grad_out(n, carry):
+        cols = pl.ds(pl.multiple_of(n * 256, 256), 256)
+        grad = dot(s.att_t[...], s.wide[:, cols]).astype(BF)
+        s.wout[:, :, :, :, :, cols] = grad.reshape(4, 2, 2, 2, 32, 256)
+        return carry
+
+    lax.fori_loop(0, 4, grad_out, 0)
+    core_copy(7, s.wout.at[:, :, :, o], s.outx).start()
+    step(2)
+    core_copy(5, s.out_acc.at[o], s.cross.at[1]).wait_recv()
+
+    def result_tile(i, carry):
+        rows = pl.ds(pl.multiple_of(i * 128, 128), 128)
+        total = s.middle[rows] + s.out_acc[r, rows] + s.cross[1, rows] + vec_row(7)
+        result_ref[rows] = total.astype(BF)
+        return carry
+
+    lax.fori_loop(0, 3, result_tile, 0)
+    core_copy(6, s.ba_all.at[o], s.ba_all.at[o]).wait_recv()
+    step(3)
+
+    def attend_back(hp, carry):
+        k_t = flip(s.qkv[1, hp])
+        dims = pl.ds(pl.multiple_of(hp * 128, 128), 128)
+        s.dkv[...] = jnp.zeros_like(s.dkv)
+        for rb in range(6):
+            keys = key_count(rb)
+            rows = slice(rb * 128, (rb + 1) * 128)
+            both = pair_rows(s.qkv[0, hp, rows])
+            at = (rb % 3) * 128
+            up = pair_rows(s.ba_all[rb // 3, at : at + 128, dims])
+            scores = dot_nt(s.qkv[1, hp, 0:keys], both) * factor + pair_mask(keys, rb)
+            probs = jnp.exp2(scores - s.lse[hp, rb, 0:1])
+            back_probs = dot_nt(s.qkv[2, hp, 0:keys], up)
+            weighted = probs * back_probs
+            centre_row = jnp.sum(weighted, axis=0, keepdims=True)
+            back_scores = (weighted - probs * centre_row).astype(BF)
+            s.dkv[1, 0:keys] += dot(probs.astype(BF), up)
+            s.dkv[0, 0:keys] += dot(back_scores, both)
+            query = dot(k_t[:, 0:keys], back_scores)
+            query = jnp.concatenate([query[0:64, 0:128], query[64:128, 128:256]], axis=0)
+            s.ffb[0, rows, dims] = (query.T * HD**-0.5).astype(BF)
+        s.ffb[1, :, dims] = (s.dkv[0] * HD**-0.5).astype(BF)
+        s.ffb[2, :, dims] = s.dkv[1].astype(BF)
+        return carry
+
+    for hp in range(4):
+        lax.fori_loop(hp, hp + 1, attend_back, 0)
+        step(4 + hp)
+
+    core_copy(5, s.out_acc.at[o], s.cross.at[1]).wait_send()
+
+    def back_in(n, carry):
+        cols = pl.ds(pl.multiple_of(n * 256, 256), 256)
+        total = dot_nt(s.ffb[0], s.win[0, n].reshape(256, 512))
+        total = total + dot_nt(s.ffb[1], s.win[1, n].reshape(256, 512))
+        total = total + dot_nt(s.ffb[2], s.win[2, n].reshape(256, 512))
+        s.out_acc[:, :, cols] = total.reshape(2, 384, 256)
+        return carry
+
+    lax.fori_loop(0, 4, back_in, 0)
+    core_copy(8, s.out_acc.at[o], s.cross.at[0]).start()
+    for i in range(3):
+        sent(ag_in(i))
+
+        def grad_in(n, carry, i=i):
+            cols = pl.ds(pl.multiple_of(n * 256, 256), 256)
+            grad = dot(s.n1t[...], s.ffb[i, :, cols]).astype(BF)
+            s.win[i, :, :, :, :, cols] = grad.reshape(4, 2, 2, 64, 256)
+            return carry
+
+        lax.fori_loop(0, 2, grad_in, 0)
+
+    core_copy(7, s.outx, s.outx).wait_recv()
+
+    def add_out(i, carry):
+        for yy in range(2):
+            for xx in range(2):
+                total = s.wout[i, yy, xx, r].astype(F32) + s.outx[i, yy, xx].astype(F32)
+                s.wout[i, yy, xx, r] = total.astype(BF)
+        return carry
+
+    lax.fori_loop(0, 4, add_out, 0)
+    step(8)
+    step(9)
+    step(10)
+
+    core_copy(8, s.out_acc.at[o], s.cross.at[0]).wait_recv()
+
+    def frame_back(i, carry):
+        rows = pl.ds(pl.multiple_of(i * 128, 128), 128)
+        unit, rate = centre(s.frames_all[r, rows].astype(F32))
+        upstream = s.out_acc[r, rows] + s.cross[0, rows]
+        back = s.bn_acc[r, rows] + norm_back(unit, rate, vec_row(0), upstream)
+        fgrad_ref[rows] = back.astype(BF)
+        gain_t, shift_t = carry
+        return (
+            gain_t + jnp.sum(upstream * unit, axis=0, keepdims=True),
+            shift_t + jnp.sum(upstream, axis=0, keepdims=True),
+        )
+
+    gain_t, shift_t = lax.fori_loop(0, 3, frame_back, (zero_row,) * 2)
+    s.gvec[0:1] = gain_t
+    s.gvec[1:2] = shift_t
+    s.gvec[2:4] = jnp.zeros((2, 1024), F32)
+    s.gvec[2:3, my_half] = jnp.sum(s.ffb[0].astype(F32), axis=0, keepdims=True)
+    s.gvec[3:4, my_half] = jnp.sum(s.ffb[2].astype(F32), axis=0, keepdims=True)
+    s.sg[...] = jnp.zeros_like(s.sg)
+    for zz in range(4):
+        for yy in range(2):
+            for xx in range(2):
+                at = (zz * 2 + yy) * 128
+                s.sg[zz, yy, xx, 0:8] = s.gvec[:, at : at + 128]
+                at = (yy * 2 + xx) * 128
+                s.sg[zz, yy, xx, 8:9] = s.gexp[zz, 0:1, at : at + 128]
+
+    for i in range(11, len(order) + 4):
+        step(i)
+
+    for item in pre:
+        item.wait_send()
+    sent(i_small)
+    core_copy(1, s.half_t.at[o], s.half_t.at[o]).wait_send()
+    core_copy(3, s.n_all.at[r], s.n_all.at[r]).wait_send()
+    core_copy(4, s.bn_acc.at[o], s.cross.at[0]).wait_send()
+    core_copy(6, s.half.at[o], s.ba_all.at[r]).wait_send()
+    core_copy(7, s.wout.at[:, :, :, o], s.outx).wait_send()
+    core_copy(8, s.out_acc.at[o], s.cross.at[0]).wait_send()
+    for it in order:
+        all_sent(it)
+
+
+def fused_shards(
+    frames, frames_cotangent, phoneme_len, prompt_len, target_segment, first_gain, first_shift, inward_weight,
+    query_bias, value_bias, outward_weight, outward_bias, second_gain, second_shift, expand_weight, expand_bias,
+    reduce_weight, reduce_bias,
+):
+    number = lax.axis_index("dp") * 2 + lax.axis_index("role")
+    quarter = number % 4
+    rows = jnp.stack(
+        [first_gain, first_shift, query_bias, value_bias, outward_bias, second_gain, second_shift, reduce_bias]
+    )
+    lane = jnp.arange(128) // 32
+    rows = jnp.where(lane[None] == quarter, jnp.tile(rows, (1, 4)), jnp.zeros((), BF))
+    small = jnp.concatenate([rows, expand_bias[None], jnp.zeros((7, 128), BF)], axis=0)
+
+    scratch = scratch_list()
+    vmem = pl.BlockSpec(memory_space=pltpu.VMEM)
+    smem = pl.BlockSpec(memory_space=pltpu.SMEM)
+    hbm = pl.BlockSpec(memory_space=pl.ANY)
+    outs = pl.pallas_call(
+        functools.partial(layer_kernel, tuple(scratch)),
+        out_shape=[
+            jax.ShapeDtypeStruct((384, 1024), BF),
+            jax.ShapeDtypeStruct((384, 1024), BF),
+            jax.ShapeDtypeStruct((32, 3072), F32),
+            jax.ShapeDtypeStruct((32, 1024), F32),
+            jax.ShapeDtypeStruct((32, 4096), F32),
+            jax.ShapeDtypeStruct((128, 1024), F32),
+            jax.ShapeDtypeStruct((16, 128), F32),
+        ],
+        in_specs=[smem, smem, vmem, hbm, hbm] + [vmem] * 5,
+        out_specs=[vmem] * 7,
+        scratch_shapes=list(scratch.values()),
+        compiler_params=pltpu.CompilerParams(
+            collective_id=0, has_side_effects=True, vmem_limit_bytes=62 * 1024 * 1024
+        ),
+    )(
+        phoneme_len, prompt_len, target_segment, frames[0], frames_cotangent[0], small, inward_weight,
+        outward_weight, expand_weight, reduce_weight,
+    )
+    result, frames_gradient, d_in, d_out, d_exp, d_red, d_small = outs
+    mine = lax.dynamic_slice(d_small, (0, quarter * 32), (8, 32))
+    return (
+        result[None], frames_gradient[None], mine[0], mine[1], d_in, mine[2], mine[3], d_out, mine[4], mine[5],
+        mine[6], d_exp, d_small[8], d_red, mine[7],
+    )
 
 
 def passed_along(block, axis, distance):
@@ -41,7 +974,7 @@
     )
 
 
-def shards(
+def plain_shards(
     frames,
     frames_cotangent,
     phoneme_len,
@@ -273,8 +1206,9 @@
         P(("dp", "role"), None),
         P(("dp", "role")),
     )
+    fused = mesh.shape["dp"] == 16 and mesh.shape["role"] == 2
     return jax.shard_map(
-        shards,
+        fused_shards if fused else plain_shards,
         mesh=mesh,
         in_specs=placed,
         out_specs=(

time: 1050 us -> 294 us (0.28); the launches traced: 1040 us -> 293 us
  waiting for transfers between devices: 520 us -> 0 us
  matrix products: 286 us -> 0 us
  Pallas kernels: 0 us -> 280 us
  blocking collectives: 126 us -> 0 us
  local copies, waits for them, and re-layouts: 41.6 us -> 10.3 us
  loops' own time: 22.1 us -> 0 us
  other arithmetic: 20.8 us -> 0.68 us
  between operations: 16.2 us -> 2.07 us
    reduce_scatter x4 -> x0, waiting for transfers between devices: 436 us -> none  [the longest x1 187 us: shards(): lax.psum_scatter(reduce_weight_term, ('dp', 'role'), scatter_dimension=0,...]
    dot_general x124 -> x0, matrix products: 286 us -> none  [the longest x52 107 us: outer_cols(): lax.dot_general(left, right, (((1,), (1,)), ((), ())), preferred_element_...]
    pallas_call x0 -> x1, Pallas kernels: none -> 280 us  [fused_shards(): pl.pallas_call(functools.partial(layer_kernel, tuple(scratch)), out_shape...]
    unnamed x2 -> x0, blocking collectives: 84.6 us -> none
    all_gather x4 -> x0, waiting for transfers between devices: 80.3 us -> none  [the longest x1 56.2 us: shards(): lax.all_gather(reduce_weight, ('dp', 'role'), axis=0, tiled=True)]
    all_gather x1 -> x0, blocking collectives: 40.9 us -> none  [shards(): lax.all_gather(expand_bias, ('dp', 'role'), axis=0, tiled=True)]
    another operation x2 -> x0, loops' own time: 22.1 us -> none  [the longest x1 11.1 us: shards(): head_outs, log_totals = lax.map(attend, jnp.arange(H))]
    dynamic_slice x48 -> x1, local copies, waits for them, and re-layouts: 19.2 us -> 0.07 us  [fused_shards(): mine = lax.dynamic_slice(d_small, (0, quarter * 32), (8, 32))]
  transfers between devices with their start and end apart: 12 -> 0, of which waited for: 6 -> 0; matrix products, arithmetic and copies ran while one was open for 31% -> 0% of each run, Pallas kernels for 0% -> 0%
where the time goes in v1:
time: 294 us; the launch traced here: 293 us
  Pallas kernels  280 us (95%)
  local copies, waits for them, and re-layouts  10.3 us (4%)
    pallas_call x1, Pallas kernels, fused_shards(): pl.pallas_call(functools.partial(layer_kernel, tuple(scratch)), out_shape...  280 us
    unnamed x36, local copies, waits for them, and re-layouts  9 us

profile of v1, /device:TPU:1, one launch (start us, length us, event | category | flops | bytes accessed | tf_op | source)
XLA Modules:
  0.0 293.4 jit_solution(15206510974671109758)
XLA Ops:
  2.0 0.0 copy-start.14
  2.0 0.0 copy-start.10
  2.0 0.0 copy-start.11
  2.0 0.0 copy-start.12
  2.0 0.0 copy-start.13
  2.0 0.0 copy-start.7
  2.1 0.0 copy-start.8
  2.1 0.0 copy-start.9
  2.1 0.1 pad.2.clone
  2.2 0.5 copy-done.14
  2.6 0.0 copy-done.10
  2.6 0.0 copy-done.11
  2.7 0.0 copy-done.12
  2.7 0.0 copy-done.13
  2.7 0.0 copy-done.7
  2.7 0.0 copy-done.8
  2.7 0.0 copy-done.9
  2.8 0.1 tile.10
  2.9 0.0 copy-start.6
  2.9 0.6 copy-done.6
  3.5 0.7 maximum_maximum_fusion.refs_5_
  4.2 280.3 %shard_map.289 = (bf16[384,1024]{1,0:T(8,128)(2,1)}, bf16[384,1024]{1,0:T(8,128)(2,1)}, f32[32,3072]{1,0:T(8,128)}, f32[32,1024]{1,0:T(8,128)}, f32[32,4096]{1,0...) custom-call(s32[1]{0:T(128)S(6)} %copy.39.refs_0_, s32[1]{0:T(128)S(6)} %copy.40.refs_1_, s32[1,384]{1,0:T(1,128)} %refs_2_.1, ...), custom_call_target="tpu_custom_call" | custom-call | tf_op jit(solution)/shard_map/pallas_call | solution.py:919
  284.5 0.0 copy-start.5
  284.5 0.7 copy-done.5
  285.2 0.5 slice_bitcast_fusion.1
  285.7 0.1 constant_dynamic-slice_fusion
  285.8 0.5 slice_bitcast_fusion
  286.4 0.0 copy-start
  286.4 2.1 copy.41
  288.5 0.0 copy-done
  288.5 0.0 copy-start.3
  288.5 0.9 copy.42
  289.4 0.4 copy-done.3
  289.7 0.0 copy-start.4
  289.7 0.0 copy-start.2
  289.7 0.7 copy.43
  290.5 0.2 copy-done.4
  290.7 0.7 copy.44
  291.4 0.0 copy-done.2
  291.4 0.0 copy-start.1
  291.4 0.8 copy.45
  292.2 0.4 copy-done.1
  292.6 0.8 copy.46
  (5 shorter events, 0.1 us)
Async XLA Ops:
  2.0 0.7 copy-start.14
  2.0 0.7 copy-start.10
  2.0 0.7 copy-start.11
  2.0 0.7 copy-start.12
  2.0 0.7 copy-start.13
  2.0 0.7 copy-start.7
  2.1 0.7 copy-start.8
  2.1 0.7 copy-start.9
  2.9 0.7 copy-start.6
  284.5 0.7 copy-start.5
  286.4 2.1 copy-start
  288.5 1.2 copy-start.3
  289.7 1.0 copy-start.4
  289.7 1.7 copy-start.2
  291.4 1.2 copy-start.1

commit v2 on v1

--- a/solution.py
+++ b/solution.py
@@ -44,7 +44,8 @@
     return rate * (pulled - first - unit * second)
 
 
-SLOTS = 3
+SLOTS = 4
+LEAD = 1
 
 
 def scratch_list():
@@ -59,7 +60,7 @@
         n_all=v((2, 384, 1024), BF),
         n1t=v((1024, 768), BF),
         n2t=v((1024, 768), BF),
-        win=v((3, 4, 2, 2, 64, 512), BF),
+        win=v((6, 4, 2, 2, 64, 256), BF),
         wout=v((4, 2, 2, 2, 32, 1024), BF),
         wexp=v((4, 4, 2, 2, 64, 512), BF),
         wred=v((4, 2, 2, 128, 1024), BF),
@@ -83,10 +84,11 @@
         gexp=v((4, 8, 512), F32),
         outx=v((4, 2, 2, 32, 1024), BF),
         rb=v((SLOTS, 2, 4, 64, 512), BF),
-        ra=v((SLOTS, 4, 64, 512), BF),
-        rz=v((7, 3, 64, 512), BF),
+        ra=v((3, 4, 64, 512), BF),
+        rz=v((4, 3, 64, 512), BF),
+        rz_in=v((6, 3, 64, 256), BF),
         rb_red=v((SLOTS, 2, 128, 1024), BF),
-        ra_red=v((SLOTS, 128, 1024), BF),
+        ra_red=v((3, 128, 1024), BF),
         rz_red=v((3, 128, 1024), BF),
         rb_out=v((2, 4, 32, 1024), BF),
         ra_out=v((4, 32, 1024), BF),
@@ -95,29 +97,31 @@
         rb_sg=v((2, 4, 16, 128), F32),
         ra_sg=v((4, 16, 128), F32),
         rz_sg=v((3, 16, 128), F32),
-        fin=v((7, 64, 512), F32),
-        fin_in=v((7, 32, 512), F32),
+        fin=v((4, 64, 512), F32),
+        fin_in=v((4, 32, 512), F32),
+        fin_w=v((6, 64, 256), F32),
+        fin_w_in=v((6, 32, 256), F32),
         sfin=v((16, 128), F32),
         sfin_in=v((16, 128), F32),
         own_s=dma((2,)),
-        pre_s=dma((10,)),
-        pre_r=dma((10,)),
-        agz_s=dma((13, 3)),
-        agz_r=dma((13, 3)),
-        aga_s=dma((13,)),
-        aga_r=dma((13,)),
-        agb_s=dma((13, 2)),
-        agb_r=dma((13, 2)),
+        pre_s=dma((13,)),
+        pre_r=dma((13,)),
+        agz_s=dma((16, 3)),
+        agz_r=dma((16, 3)),
+        aga_s=dma((16,)),
+        aga_r=dma((16,)),
+        agb_s=dma((16, 2)),
+        agb_r=dma((16, 2)),
         core_s=dma((9,)),
         core_r=dma((9,)),
-        rsb_s=dma((13, 2)),
-        rsb_r=dma((13, 2)),
-        rsa_s=dma((13,)),
-        rsa_r=dma((13,)),
-        rsz_s=dma((13, 3)),
-        rsz_r=dma((13, 3)),
-        fin_s=dma((8,)),
-        fin_r=dma((8,)),
+        rsb_s=dma((16, 2)),
+        rsb_r=dma((16, 2)),
+        rsa_s=dma((16,)),
+        rsa_r=dma((16,)),
+        rsz_s=dma((16, 3)),
+        rsz_r=dma((16, 3)),
+        fin_s=dma((11,)),
+        fin_r=dma((11,)),
     )
 
 
@@ -162,8 +166,8 @@
     my_rows = pl.ds(pl.multiple_of(r * 32, 32), 32)
     o_rows = pl.ds(pl.multiple_of(o * 32, 32), 32)
 
-    def half_cols(section, who):
-        return pl.ds(pl.multiple_of(section * 1024 + who * 512, 512), 512)
+    def part_cols(part, who):
+        return pl.ds(pl.multiple_of((part // 2) * 1024 + who * 512 + (part % 2) * 256, 256), 256)
 
     for block in range(16):
         for who in range(2):
@@ -172,28 +176,28 @@
             ]
     pre = []
     pre.append(copy(small_in, s.small.at[z, y, x, r], s.pre_s.at[0], s.pre_r.at[0], core_dev))
-    for i in range(3):
+    for i in range(6):
         pre.append(
             copy(
-                win_in.at[:, half_cols(i, o)],
+                win_in.at[:, part_cols(i, o)],
                 s.win.at[i, z, y, x, my_rows],
                 s.pre_s.at[1 + i],
                 s.pre_r.at[1 + i],
                 core_dev,
             )
         )
-    pre.append(copy(frames_ref, s.frames_all.at[r], s.pre_s.at[4], s.pre_r.at[4], core_dev))
+    pre.append(copy(frames_ref, s.frames_all.at[r], s.pre_s.at[7], s.pre_r.at[7], core_dev))
     for j in range(4):
         pre.append(
             copy(
                 s.stage.at[o, :, pl.ds(j * 512, 512)],
                 s.wexp.at[j, z, y, x, my_rows],
-                s.pre_s.at[5 + j],
-                s.pre_r.at[5 + j],
+                s.pre_s.at[8 + j],
+                s.pre_r.at[8 + j],
                 core_dev,
             )
         )
-    pre.append(copy(cot_ref, s.c_all.at[r], s.pre_s.at[9], s.pre_r.at[9], core_dev))
+    pre.append(copy(cot_ref, s.c_all.at[r], s.pre_s.at[12], s.pre_r.at[12], core_dev))
     for item in pre:
         item.start()
     own_frames = pltpu.make_async_copy(frames_ref, s.frames_all.at[r], s.own_s.at[0])
@@ -201,8 +205,8 @@
     own_frames.start()
     own_cot.start()
     s.small[z, y, x, r] = small_in[...]
-    for i in range(3):
-        s.win[i, z, y, x, my_rows] = win_in[:, half_cols(i, r)]
+    for i in range(6):
+        s.win[i, z, y, x, my_rows] = win_in[:, part_cols(i, r)]
     s.wout[z, y, x, r] = wout_in[...]
     s.wred[z, y, x] = wred_in[...]
     for j in range(4):
@@ -218,12 +222,12 @@
 
     def ag_out():
         return Bag(
-            t=4, piece=lambda a, b, c: s.wout.at[a, b, c, r], col=lambda b, c: s.wout.at[:, b, c, r], plane=None
+            t=7, piece=lambda a, b, c: s.wout.at[a, b, c, r], col=lambda b, c: s.wout.at[:, b, c, r], plane=None
         )
 
     def ag_exp(j):
         return Bag(
-            t=5 + 2 * j,
+            t=8 + 2 * j,
             piece=lambda a, b, c: s.wexp.at[j, a, b, c],
             col=lambda b, c: s.wexp.at[j, :, b, c],
             plane=None,
@@ -231,7 +235,7 @@
 
     def ag_red(j):
         return Bag(
-            t=6 + 2 * j, piece=lambda a, b, c: s.wred.at[j, b, c], col=lambda b, c: s.wred.at[j, b, c], plane=j
+            t=9 + 2 * j, piece=lambda a, b, c: s.wred.at[j, b, c], col=lambda b, c: s.wred.at[j, b, c], plane=j
         )
 
     def z_copies(it):
@@ -293,18 +297,23 @@
         b_copy(it, 0, y, x).wait_send()
         b_copy(it, 1, ya, xa).wait_send()
 
-    i_small, i_q, i_k, i_v, i_out = ag_small(), ag_in(0), ag_in(1), ag_in(2), ag_out()
+    i_small, i_out = ag_small(), ag_out()
+    i_w = [ag_in(i) for i in range(6)]
 
     def pre_in(index, dst):
         copy(dst, dst, s.pre_s.at[index], s.pre_r.at[index], core_dev).wait_recv()
 
+    def begin(i):
+        pre_in(1 + i, s.win.at[i, z, y, x, o_rows])
+        e0(i_w[i])
+
     pre_in(0, s.small.at[z, y, x, o])
     e0(i_small)
-    pre_in(1, s.win.at[0, z, y, x, o_rows])
-    e0(i_q)
+    begin(0)
+    begin(1)
     e1(i_small)
-    pre_in(2, s.win.at[1, z, y, x, o_rows])
-    e0(i_k)
+    e1(i_w[0])
+    begin(2)
 
     own_frames.wait()
     own_cot.wait()
@@ -324,12 +333,10 @@
     s.mask[0:384, 384:768] = as_bias(seen)
     s.mask[384:768, 384:768] = as_bias(causal & (seg_wide == seg_tall))
 
-    e1(i_q)
     e2(i_small)
-    pre_in(3, s.win.at[2, z, y, x, o_rows])
-    e0(i_v)
-    e1(i_k)
-    e2(i_q)
+    e1(i_w[1])
+    e2(i_w[0])
+    begin(3)
     e3(i_small)
 
     def tile_sum(q):
@@ -350,7 +357,7 @@
     def vec_row(i):
         return s.vec[i : i + 1, :]
 
-    pre_in(4, s.frames_all.at[o])
+    pre_in(7, s.frames_all.at[o])
 
     def norm_tile(i, carry):
         who, rows = i // 3, pl.ds(pl.multiple_of((i % 3) * 128, 128), 128)
@@ -362,40 +369,50 @@
 
     lax.fori_loop(0, 6, norm_tile, 0)
 
-    def project(i):
-        def body(n, carry):
-            cols = pl.ds(pl.multiple_of(n * 256, 256), 256)
-            weight = s.win[i, :, :, :, :, cols].reshape(1024, 256)
-            left = s.n_all[...].reshape(768, 1024)
-            mixed = dot(left, weight)
-            if i != 1:
-                bias_at = pl.ds(pl.multiple_of(r * 512 + n * 256, 256), 256)
-                bias_row = 2 if i == 0 else 3
-                mixed = mixed + s.vec[bias_row : bias_row + 1, bias_at]
-            mixed = mixed.astype(BF)
-            s.qkv[i, 2 * n] = mixed[:, 0:128]
-            s.qkv[i, 2 * n + 1] = mixed[:, 128:256]
-            return carry
-
-        lax.fori_loop(0, 2, body, 0)
-
+    def project(part):
+        section, n = part // 2, part % 2
+        mixed = dot(s.n_all[...].reshape(768, 1024), s.win[part].reshape(1024, 256))
+        if section != 1:
+            bias_at = pl.ds(pl.multiple_of(r * 512 + n * 256, 256), 256)
+            bias_row = 2 if section == 0 else 3
+            mixed = mixed + s.vec[bias_row : bias_row + 1, bias_at]
+        mixed = mixed.astype(BF)
+        s.qkv[section, 2 * n] = mixed[:, 0:128]
+        s.qkv[section, 2 * n + 1] = mixed[:, 128:256]
+
+    e1(i_w[2])
+    e2(i_w[1])
+    begin(4)
+    e3(i_w[0])
+    project(0)
+    e1(i_w[3])
+    e2(i_w[2])
+    begin(5)
+    e3(i_w[1])
+    project(1)
+    e1(i_w[4])
+    e2(i_w[3])
     e0(i_out)
-    e1(i_v)
-    e2(i_k)
-    e3(i_q)
-    project(0)
+    e3(i_w[2])
+    project(2)
     for j in range(4):
-        pre_in(5 + j, s.wexp.at[j, z, y, x, o_rows])
+        pre_in(8 + j, s.wexp.at[j, z, y, x, o_rows])
+    e1(i_w[5])
+    e2(i_w[4])
     e0(ag_exp(0))
+    e3(i_w[3])
+    project(3)
     e1(i_out)
-    e2(i_v)
-    e3(i_k)
-    project(1)
+    e2(i_w[5])
     e0(ag_red(0))
+    e3(i_w[4])
+    project(4)
     e1(ag_exp(0))
     e2(i_out)
-    e3(i_v)
-    project(2)
+    e3(i_w[5])
+    project(5)
+    e0(ag_exp(1))
+    e1(ag_red(0))
 
     factor = HD**-0.5 * LOG2E
     low_lane = lax.broadcasted_iota(jnp.int32, (128, 128), 1) < 64
@@ -441,8 +458,6 @@
     core_copy(1, s.half_t.at[o], s.att_t.at[my_half]).start()
     s.wide[:, my_half] = s.half[r]
     s.att_t[my_half] = s.half_t[r]
-    e0(ag_exp(1))
-    e1(ag_red(0))
     e2(ag_exp(0))
     e3(i_out)
     out_swap = core_copy(2, s.wout.at[:, :, :, r], s.wout.at[:, :, :, r])
@@ -450,6 +465,9 @@
     core_copy(0, s.wide.at[:, o_half], s.wide.at[:, o_half]).wait_recv()
     core_copy(1, s.att_t.at[o_half], s.att_t.at[o_half]).wait_recv()
     core_copy(2, s.wout.at[:, :, :, o], s.wout.at[:, :, :, o]).wait_recv()
+    e0(ag_red(1))
+    e1(ag_exp(1))
+    e2(ag_red(0))
 
     def out_tile(n, carry):
         cols = pl.ds(pl.multiple_of(n * 256, 256), 256)
@@ -467,7 +485,7 @@
 
     lax.fori_loop(0, 3, norm_two, 0)
     core_copy(3, s.n_all.at[r], s.n_all.at[r]).start()
-    pre_in(9, s.c_all.at[o])
+    pre_in(12, s.c_all.at[o])
     s.out_acc[...] = jnp.zeros_like(s.out_acc)
     s.bn_acc[...] = jnp.zeros_like(s.bn_acc)
     core_copy(3, s.n_all.at[o], s.n_all.at[o]).wait_recv()
@@ -479,29 +497,214 @@
 
     lax.fori_loop(0, 6, flip_two, 0)
 
-    def feed(j, carry):
-        more = j < 3
-
-        @pl.when(more)
-        def _():
-            e0(ag_red(j + 1))
-            e1(ag_exp(j + 1))
-
-        e2(ag_red(j))
-        e3(ag_exp(j))
-
-        @pl.when(j < 2)
-        def _():
-            e0(ag_exp(j + 2))
-
-        @pl.when(more)
-        def _():
+    def rs_exp(j):
+        return Bag(
+            t=j, fin=j, parts=4, plane=None, piece=lambda a, b, c: s.wexp.at[j, a, b, c],
+            col=lambda b, c: s.wexp.at[j, :, b, c], rb=lambda w: s.rb.at[j % SLOTS, w], ra=s.ra.at[j % 3],
+            rz=lambda k: s.rz.at[j, k],
+        )
+
+    def rs_in(i):
+        slot, part = ((0, 0), (1, 0), (0, 1), (1, 1), (2, 0), (2, 1))[i]
+        half = slice(256 * part, 256 * part + 256)
+        again = slice(256 * (i % 2), 256 * (i % 2) + 256)
+        return Bag(
+            t=9 + i, fin=4 + i, parts=4, plane=None, piece=lambda a, b, c: s.win.at[i, a, b, c],
+            col=lambda b, c: s.win.at[i, :, b, c], rb=lambda w: s.rb.at[slot, w, :, :, half],
+            ra=s.ra.at[(1, 2, 0)[i // 2], :, :, again], rz=lambda k: s.rz_in.at[i, k],
+        )
+
+    def rs_red(j):
+        return Bag(
+            t=4 + j, fin=None, parts=1, plane=j, piece=lambda a, b, c: s.wred.at[j, b, c],
+            col=lambda b, c: s.wred.at[j, b, c], rb=lambda w: s.rb_red.at[j % SLOTS, w],
+            ra=s.ra_red.at[j % 3], rz=lambda k: s.rz_red.at[k],
+        )
+
+    def rs_out():
+        return Bag(
+            t=8, fin=None, parts=4, plane=None, piece=lambda a, b, c: s.wout.at[a, b, c, r],
+            col=lambda b, c: s.wout.at[:, b, c, r], rb=lambda w: s.rb_out.at[w], ra=s.ra_out,
+            rz=lambda k: s.rz_out.at[k],
+        )
+
+    def rs_small():
+        return Bag(
+            t=15, fin=None, parts=4, plane=None, piece=lambda a, b, c: s.sg.at[a, b, c],
+            col=lambda b, c: s.sg.at[:, b, c], rb=lambda w: s.rb_sg.at[w], ra=s.ra_sg,
+            rz=lambda k: s.rz_sg.at[k],
+        )
+
+    def rb_copy(it, which, yy, xx):
+        return copy(it.col(yy, xx), it.rb(which), s.rsb_s.at[it.t, which], s.rsb_r.at[it.t, which], b_dev)
+
+    def ra_copy(it):
+        return copy(it.col(ya, xa), it.ra, s.rsa_s.at[it.t], s.rsa_r.at[it.t], a_dev)
+
+    def rz_copy(it, k, at):
+        return copy(it.piece(at, y, x), it.rz(k), s.rsz_s.at[it.t, k], s.rsz_r.at[it.t, k], z_dev[k])
+
+    def add_into(it, yy, xx, sources):
+        target = it.col(yy, xx)
+        kind = F32 if it.t == 15 else BF
+
+        def one(at):
+            total = target[at].astype(F32)
+            for src in sources:
+                total = total + src[at].astype(F32)
+            target[at] = total.astype(kind)
+
+        if it.parts == 4:
+
+            def body(i, carry):
+                one(i)
+                return carry
+        else:
+
+            def body(i, carry):
+                one(pl.ds(pl.multiple_of(i * 32, 32), 32))
+                return carry
+
+        lax.fori_loop(0, 4, body, 0)
+
+    def f0(it):
+        rb_copy(it, 0, yc, xc).start()
+        rb_copy(it, 1, yb, xb).start()
+
+    def f1(it):
+        rb_copy(it, 0, yc, xc).wait_recv()
+        add_into(it, ya, xa, [it.rb(0)])
+        ra_copy(it).start()
+
+    def f2(it):
+        rb_copy(it, 1, yb, xb).wait_recv()
+        ra_copy(it).wait_recv()
+        add_into(it, y, x, [it.rb(1), it.ra])
+
+        if it.plane is None:
+            for k in range(3):
+                rz_copy(it, k, z_at[k]).start()
+        else:
+
+            @pl.when(z != it.plane)
+            def _():
+                k = (it.plane + 4 - z) % 4 - 1
+                copy(
+                    it.piece(z, y, x), it.rz(k), s.rsz_s.at[it.t, k], s.rsz_r.at[it.t, k],
+                    (it.plane * 4 + y * 2 + x, r),
+                ).start()
+
+    def z_total(it):
+        for k in range(3):
+            rz_copy(it, k, z_at[k]).wait_recv()
+        total = it.piece(z, y, x)[...].astype(F32)
+        for k in range(3):
+            total = total + it.rz(k)[...].astype(F32)
+        return total
+
+    def fin_refs(index):
+        if index < 4:
+            return s.fin.at[index], s.fin_in.at[index]
+        return s.fin_w.at[index - 4], s.fin_w_in.at[index - 4]
+
+    def fin_copy(index):
+        out, back = fin_refs(index)
+        return copy(out.at[o_rows], back, s.fin_s.at[index], s.fin_r.at[index], core_dev)
+
+    def small_fin():
+        return copy(s.sfin, s.sfin_in, s.fin_s.at[10], s.fin_r.at[10], core_dev)
+
+    def put(index, value, who):
+        if index < 4:
+            for i in range(4):
+                at = pl.ds(pl.multiple_of((2 * (4 * index + i) + who) * 128, 128), 128)
+                dwexp_ref[:, at] = value[:, i * 128 : (i + 1) * 128]
+        else:
+            dwin_ref[:, part_cols(index - 4, who)] = value
+
+    def f4(it):
+        if it.plane is not None:
+
+            @pl.when(z == it.plane)
+            def _():
+                dwred_ref[...] = z_total(it)
+        elif it.t == 8:
+            dwout_ref[...] = z_total(it)
+        elif it.t == 15:
+            s.sfin[...] = z_total(it)
+            small_fin().start()
+        else:
+            out, _ = fin_refs(it.fin)
+            out[...] = z_total(it)
+            fin_copy(it.fin).start()
+            put(it.fin, out[my_rows], r)
+
+    def f5(it):
+        if it.fin is not None:
+            fin_copy(it.fin).wait_recv()
+            put(it.fin, fin_refs(it.fin)[1][...], o)
+        elif it.t == 15:
+            small_fin().wait_recv()
+            row = lax.broadcasted_iota(jnp.int32, (16, 128), 0)
+            own = s.sfin[...]
+            dsmall_ref[...] = jnp.where(row < 8, own + s.sfin_in[...], own)
+
+    def all_sent(it):
+        rb_copy(it, 0, yc, xc).wait_send()
+        rb_copy(it, 1, yb, xb).wait_send()
+        ra_copy(it).wait_send()
+        if it.plane is None:
+            for k in range(3):
+                rz_copy(it, k, z_at[k]).wait_send()
+        else:
+
+            @pl.when(z != it.plane)
+            def _():
+                k = (it.plane + 4 - z) % 4 - 1
+                copy(
+                    it.piece(z, y, x), it.rz(k), s.rsz_s.at[it.t, k], s.rsz_r.at[it.t, k],
+                    (it.plane * 4 + y * 2 + x, r),
+                ).wait_send()
+        if it.fin is not None:
+            fin_copy(it.fin).wait_send()
+        elif it.t == 15:
+            small_fin().wait_send()
+
+    order = []
+    for j in range(4):
+        order += [rs_red(j), rs_exp(j)]
+    order += [rs_out()] + [rs_in(i) for i in range(6)] + [rs_small()]
+
+    def step(i):
+        for event, lag in ((f0, -LEAD), (f1, 1), (f2, 2), (f4, 3), (f5, 4)):
+            if 0 <= i - lag < len(order):
+                event(order[i - lag])
+
+    def when(cond, go):
+        if isinstance(cond, bool):
+            if cond:
+                go()
+        else:
+            pl.when(cond)(go)
+
+    def feed(j, between):
+        def ahead_one():
             e1(ag_red(j + 1))
             e2(ag_exp(j + 1))
 
+        def ahead_two():
+            e0(ag_red(j + 2))
+            e1(ag_exp(j + 2))
+
+        when(j < 2, lambda: e0(ag_exp(j + 2)))
+        when(j < 3, ahead_one)
+        e3(ag_exp(j))
+        when(j < 2, ahead_two)
+        when(j < 3, lambda: e2(ag_red(j + 1)))
         e3(ag_red(j))
         sent(ag_exp(j))
         sent(ag_red(j))
+        between(0)
 
         def hidden(n, inside):
             cols = pl.ds(pl.multiple_of(n * 256, 256), 256)
@@ -529,6 +732,7 @@
             return inside
 
         lax.fori_loop(0, 4, wide_tile, 0)
+        between(1)
 
         def grad_red(n, inside):
             cols = pl.ds(pl.multiple_of(n * 256, 256), 256)
@@ -545,186 +749,28 @@
             return inside
 
         lax.fori_loop(0, 2, grad_exp, 0)
+        between(2)
+
+    def early_feed(j, carry):
+        feed(j, lambda place: None)
         return carry
 
-    lax.fori_loop(0, 4, feed, 0)
-
-    def rs_exp(j):
-        return Bag(
-            t=j, fin=j, parts=4, plane=None, piece=lambda a, b, c: s.wexp.at[j, a, b, c],
-            col=lambda b, c: s.wexp.at[j, :, b, c], rb=lambda w: s.rb.at[j % SLOTS, w], ra=s.ra.at[j % SLOTS],
-            rz=lambda k: s.rz.at[j, k],
-        )
-
-    def rs_in(i):
-        return Bag(
-            t=9 + i, fin=4 + i, parts=4, plane=None, piece=lambda a, b, c: s.win.at[i, a, b, c],
-            col=lambda b, c: s.win.at[i, :, b, c], rb=lambda w: s.rb.at[(4 + i) % SLOTS, w],
-            ra=s.ra.at[(4 + i) % SLOTS], rz=lambda k: s.rz.at[4 + i, k],
-        )
-
-    def rs_red(j):
-        return Bag(
-            t=4 + j, fin=None, parts=1, plane=j, piece=lambda a, b, c: s.wred.at[j, b, c],
-            col=lambda b, c: s.wred.at[j, b, c], rb=lambda w: s.rb_red.at[j % SLOTS, w],
-            ra=s.ra_red.at[j % SLOTS], rz=lambda k: s.rz_red.at[k],
-        )
-
-    def rs_out():
-        return Bag(
-            t=8, fin=None, parts=4, plane=None, piece=lambda a, b, c: s.wout.at[a, b, c, r],
-            col=lambda b, c: s.wout.at[:, b, c, r], rb=lambda w: s.rb_out.at[w], ra=s.ra_out,
-            rz=lambda k: s.rz_out.at[k],
-        )
-
-    def rs_small():
-        return Bag(
-            t=12, fin=None, parts=4, plane=None, piece=lambda a, b, c: s.sg.at[a, b, c],
-            col=lambda b, c: s.sg.at[:, b, c], rb=lambda w: s.rb_sg.at[w], ra=s.ra_sg,
-            rz=lambda k: s.rz_sg.at[k],
-        )
-
-    def rb_copy(it, which, yy, xx):
-        return copy(it.col(yy, xx), it.rb(which), s.rsb_s.at[it.t, which], s.rsb_r.at[it.t, which], b_dev)
-
-    def ra_copy(it):
-        return copy(it.col(ya, xa), it.ra, s.rsa_s.at[it.t], s.rsa_r.at[it.t], a_dev)
-
-    def rz_copy(it, k, at):
-        return copy(it.piece(at, y, x), it.rz(k), s.rsz_s.at[it.t, k], s.rsz_r.at[it.t, k], z_dev[k])
-
-    def add_into(it, yy, xx, sources):
-        target = it.col(yy, xx)
-        kind = F32 if it.t == 12 else BF
-
-        def one(at):
-            total = target[at].astype(F32)
-            for src in sources:
-                total = total + src[at].astype(F32)
-            target[at] = total.astype(kind)
-
-        if it.parts == 4:
-
-            def body(i, carry):
-                one(i)
-                return carry
+    lax.fori_loop(0, 3, early_feed, 0)
+
+    def start_reduction(place):
+        if place == 0:
+            for it in order[:LEAD]:
+                f0(it)
+            step(0)
+        elif place == 1:
+            core_copy(4, s.bn_acc.at[o], s.cross.at[0]).start()
+            core_copy(5, s.out_acc.at[o], s.cross.at[1]).start()
+            step(1)
         else:
-
-            def body(i, carry):
-                one(pl.ds(pl.multiple_of(i * 32, 32), 32))
-                return carry
-
-        lax.fori_loop(0, 4, body, 0)
-
-    def f0(it):
-        rb_copy(it, 0, yc, xc).start()
-        rb_copy(it, 1, yb, xb).start()
-
-    def f1(it):
-        rb_copy(it, 0, yc, xc).wait_recv()
-        add_into(it, ya, xa, [it.rb(0)])
-        ra_copy(it).start()
-
-    def f2(it):
-        rb_copy(it, 1, yb, xb).wait_recv()
-        ra_copy(it).wait_recv()
-        add_into(it, y, x, [it.rb(1), it.ra])
-
-        if it.plane is None:
-            for k in range(3):
-                rz_copy(it, k, z_at[k]).start()
-        else:
-
-            @pl.when(z != it.plane)
-            def _():
-                k = (it.plane + 4 - z) % 4 - 1
-                copy(
-                    it.piece(z, y, x), it.rz(k), s.rsz_s.at[it.t, k], s.rsz_r.at[it.t, k],
-                    (it.plane * 4 + y * 2 + x, r),
-                ).start()
-
-    def z_total(it):
-        for k in range(3):
-            rz_copy(it, k, z_at[k]).wait_recv()
-        total = it.piece(z, y, x)[...].astype(F32)
-        for k in range(3):
-            total = total + it.rz(k)[...].astype(F32)
-        return total
-
-    def fin_copy(index):
-        return copy(s.fin.at[index, o_rows], s.fin_in.at[index], s.fin_s.at[index], s.fin_r.at[index], core_dev)
-
-    def small_fin():
-        return copy(s.sfin, s.sfin_in, s.fin_s.at[7], s.fin_r.at[7], core_dev)
-
-    def put(index, value, who):
-        if index < 4:
-            for i in range(4):
-                at = pl.ds(pl.multiple_of((2 * (4 * index + i) + who) * 128, 128), 128)
-                dwexp_ref[:, at] = value[:, i * 128 : (i + 1) * 128]
-        else:
-            dwin_ref[:, half_cols(index - 4, who)] = value
-
-    def f4(it):
-        if it.plane is not None:
-
-            @pl.when(z == it.plane)
-            def _():
-                dwred_ref[...] = z_total(it)
-        elif it.t == 8:
-            dwout_ref[...] = z_total(it)
-        elif it.t == 12:
-            s.sfin[...] = z_total(it)
-            small_fin().start()
-        else:
-            s.fin[it.fin] = z_total(it)
-            fin_copy(it.fin).start()
-            put(it.fin, s.fin[it.fin, my_rows], r)
-
-    def f5(it):
-        if it.fin is not None:
-            fin_copy(it.fin).wait_recv()
-            put(it.fin, s.fin_in[it.fin], o)
-        elif it.t == 12:
-            small_fin().wait_recv()
-            row = lax.broadcasted_iota(jnp.int32, (16, 128), 0)
-            own = s.sfin[...]
-            dsmall_ref[...] = jnp.where(row < 8, own + s.sfin_in[...], own)
-
-    def all_sent(it):
-        rb_copy(it, 0, yc, xc).wait_send()
-        rb_copy(it, 1, yb, xb).wait_send()
-        ra_copy(it).wait_send()
-        if it.plane is None:
-            for k in range(3):
-                rz_copy(it, k, z_at[k]).wait_send()
-        else:
-
-            @pl.when(z != it.plane)
-            def _():
-                k = (it.plane + 4 - z) % 4 - 1
-                copy(
-                    it.piece(z, y, x), it.rz(k), s.rsz_s.at[it.t, k], s.rsz_r.at[it.t, k],
-                    (it.plane * 4 + y * 2 + x, r),
-                ).wait_send()
-        if it.fin is not None:
-            fin_copy(it.fin).wait_send()
-        elif it.t == 12:
-            small_fin().wait_send()
-
-    order = []
-    for j in range(4):
-        order += [rs_exp(j), rs_red(j)]
-    order += [rs_out(), rs_in(0), rs_in(1), rs_in(2), rs_small()]
-
-    def step(i):
-        for event, lag in ((f0, 0), (f1, 1), (f2, 2), (f4, 3), (f5, 4)):
-            if 0 <= i - lag < len(order):
-                event(order[i - lag])
-
-    core_copy(4, s.bn_acc.at[o], s.cross.at[0]).start()
-    core_copy(5, s.out_acc.at[o], s.cross.at[1]).start()
-    step(0)
+            step(2)
+
+    feed(3, start_reduction)
+
     core_copy(4, s.bn_acc.at[o], s.cross.at[0]).wait_recv()
 
     def middle_back(i, carry):
@@ -763,7 +809,7 @@
     lax.fori_loop(0, 4, back_att, 0)
     core_copy(6, s.half.at[o], s.ba_all.at[r]).start()
     s.ba_all[r] = s.half[r]
-    step(1)
+    step(3)
     sent(i_out)
 
     def grad_out(n, carry):
@@ -774,7 +820,6 @@
 
     lax.fori_loop(0, 4, grad_out, 0)
     core_copy(7, s.wout.at[:, :, :, o], s.outx).start()
-    step(2)
     core_copy(5, s.out_acc.at[o], s.cross.at[1]).wait_recv()
 
     def result_tile(i, carry):
@@ -785,7 +830,6 @@
 
     lax.fori_loop(0, 3, result_tile, 0)
     core_copy(6, s.ba_all.at[o], s.ba_all.at[o]).wait_recv()
-    step(3)
 
     def attend_back(hp, carry):
         k_t = flip(s.qkv[1, hp])
@@ -812,33 +856,6 @@
         s.ffb[2, :, dims] = s.dkv[1].astype(BF)
         return carry
 
-    for hp in range(4):
-        lax.fori_loop(hp, hp + 1, attend_back, 0)
-        step(4 + hp)
-
-    core_copy(5, s.out_acc.at[o], s.cross.at[1]).wait_send()
-
-    def back_in(n, carry):
-        cols = pl.ds(pl.multiple_of(n * 256, 256), 256)
-        total = dot_nt(s.ffb[0], s.win[0, n].reshape(256, 512))
-        total = total + dot_nt(s.ffb[1], s.win[1, n].reshape(256, 512))
-        total = total + dot_nt(s.ffb[2], s.win[2, n].reshape(256, 512))
-        s.out_acc[:, :, cols] = total.reshape(2, 384, 256)
-        return carry
-
-    lax.fori_loop(0, 4, back_in, 0)
-    core_copy(8, s.out_acc.at[o], s.cross.at[0]).start()
-    for i in range(3):
-        sent(ag_in(i))
-
-        def grad_in(n, carry, i=i):
-            cols = pl.ds(pl.multiple_of(n * 256, 256), 256)
-            grad = dot(s.n1t[...], s.ffb[i, :, cols]).astype(BF)
-            s.win[i, :, :, :, :, cols] = grad.reshape(4, 2, 2, 64, 256)
-            return carry
-
-        lax.fori_loop(0, 2, grad_in, 0)
-
     core_copy(7, s.outx, s.outx).wait_recv()
 
     def add_out(i, carry):
@@ -849,9 +866,36 @@
         return carry
 
     lax.fori_loop(0, 4, add_out, 0)
+
+    lax.fori_loop(0, 1, attend_back, 0)
+    step(4)
+    lax.fori_loop(1, 3, attend_back, 0)
+    step(5)
+    lax.fori_loop(3, 4, attend_back, 0)
+
+    core_copy(5, s.out_acc.at[o], s.cross.at[1]).wait_send()
+
+    def back_in(n, carry):
+        cols = pl.ds(pl.multiple_of(n * 256, 256), 256)
+        total = dot_nt(s.ffb[0, :, 0:256], s.win[0, n].reshape(256, 256))
+        for part in range(1, 6):
+            at = (part % 2) * 256
+            total = total + dot_nt(s.ffb[part // 2, :, at : at + 256], s.win[part, n].reshape(256, 256))
+        s.out_acc[:, :, cols] = total.reshape(2, 384, 256)
+        return carry
+
+    lax.fori_loop(0, 4, back_in, 0)
+    core_copy(8, s.out_acc.at[o], s.cross.at[0]).start()
+    step(6)
+    for part in range(6):
+        sent(i_w[part])
+        at = (part % 2) * 256
+        grad = dot(s.n1t[...], s.ffb[part // 2, :, at : at + 256]).astype(BF)
+        s.win[part] = grad.reshape(4, 2, 2, 64, 256)
+        if part == 2:
+            step(7)
     step(8)
     step(9)
-    step(10)
 
     core_copy(8, s.out_acc.at[o], s.cross.at[0]).wait_recv()
 
@@ -882,7 +926,7 @@
                 at = (yy * 2 + xx) * 128
                 s.sg[zz, yy, xx, 8:9] = s.gexp[zz, 0:1, at : at + 128]
 
-    for i in range(11, len(order) + 4):
+    for i in range(10, len(order) + 4):
         step(i)
 
     for item in pre:
@@ -896,6 +940,20 @@
     core_copy(8, s.out_acc.at[o], s.cross.at[0]).wait_send()
     for it in order:
         all_sent(it)
+
+
+def hand_on(*refs):
+    given, taken, held = refs[0:6], refs[6:12], refs[12:18]
+    sems = refs[18]
+    inward = [pltpu.make_async_copy(given[i], held[i], sems.at[0, i]) for i in range(6)]
+    outward = [pltpu.make_async_copy(held[i], taken[i], sems.at[1, i]) for i in range(6)]
+    for item in inward:
+        item.start()
+    for i in range(6):
+        inward[i].wait()
+        outward[i].start()
+    for item in outward:
+        item.wait()
 
 
 def fused_shards(
@@ -937,7 +995,15 @@
         phoneme_len, prompt_len, target_segment, frames[0], frames_cotangent[0], small, inward_weight,
         outward_weight, expand_weight, reduce_weight,
     )
-    result, frames_gradient, d_in, d_out, d_exp, d_red, d_small = outs
+    d_small = outs[6]
+    result, frames_gradient, d_in, d_out, d_exp, d_red = pl.pallas_call(
+        hand_on,
+        out_shape=[jax.ShapeDtypeStruct(item.shape, item.dtype) for item in outs[:6]],
+        in_specs=[hbm] * 6,
+        out_specs=[hbm] * 6,
+        scratch_shapes=[pltpu.VMEM(item.shape, item.dtype) for item in outs[:6]]
+        + [pltpu.SemaphoreType.DMA((2, 6))],
+    )(*outs[:6])
     mine = lax.dynamic_slice(d_small, (0, quarter * 32), (8, 32))
     return (
         result[None], frames_gradient[None], mine[0], mine[1], d_in, mine[2], mine[3], d_out, mine[4], mine[5],

time: 294 us -> 268 us (0.912)
  Pallas kernels: 280 us -> 262 us
  local copies, waits for them, and re-layouts: 10.3 us -> 3.29 us
    pallas_call x1, Pallas kernels: 280 us -> 259 us  [fused_shards(): pl.pallas_call(functools.partial(layer_kernel, tuple(scratch)), out_shape...]
    unnamed x36 -> x20, local copies, waits for them, and re-layouts: 9 us -> 1.95 us
where the time goes in v2:
time: 268 us
  Pallas kernels  262 us (98%)
  local copies, waits for them, and re-layouts  3.29 us (1%)
    pallas_call x1, Pallas kernels, fused_shards(): pl.pallas_call(functools.partial(layer_kernel, tuple(scratch)), out_shape...  259 us

profile of v2, /device:TPU:1, one launch (start us, length us, event | category | flops | bytes accessed | tf_op | source)
XLA Modules:
  0.0 267.6 jit_solution(13347740792704224884)
XLA Ops:
  2.0 0.0 copy-start.9
  2.0 0.0 copy-start.5
  2.0 0.0 copy-start.6
  2.0 0.0 copy-start.7
  2.0 0.0 copy-start.8
  2.0 0.0 copy-start.2
  2.1 0.0 copy-start.3
  2.1 0.0 copy-start.4
  2.1 0.1 pad.2.clone
  2.2 0.5 copy-done.9
  2.6 0.0 copy-done.5
  2.6 0.0 copy-done.6
  2.7 0.0 copy-done.7
  2.7 0.0 copy-done.8
  2.7 0.0 copy-done.2
  2.7 0.0 copy-done.3
  2.7 0.0 copy-done.4
  2.8 0.1 tile.10
  2.9 0.0 copy-start.1
  2.9 0.6 copy-done.1
  3.5 0.7 maximum_maximum_fusion.refs_5_
  4.2 258.7 %shard_map.289 = (bf16[384,1024]{1,0:T(8,128)(2,1)}, bf16[384,1024]{1,0:T(8,128)(2,1)}, f32[32,3072]{1,0:T(8,128)}, f32[32,1024]{1,0:T(8,128)}, f32[32,4096]{1,0...) custom-call(s32[1]{0:T(128)S(6)} %copy.33.refs_0_, s32[1]{0:T(128)S(6)} %copy.34.refs_1_, s32[1,384]{1,0:T(1,128)} %refs_2_.1, ...), custom_call_target="tpu_custom_call" | custom-call | tf_op jit(solution)/shard_map/pallas_call | solution.py:977
  262.9 2.9 %shard_map.290 = (bf16[384,1024]{1,0:T(8,128)(2,1)}, bf16[384,1024]{1,0:T(8,128)(2,1)}, f32[32,3072]{1,0:T(8,128)}, f32[32,1024]{1,0:T(8,128)}, f32[32,4096]{1,0:T(8,128)}, /*index=5*/f32[128,1024]{1,0:T(8,128)}) custom-call(bf16[384,1024]{1,0:T(8,128)(2,1)} %get-tuple-element.28.refs_0_, bf16[384,1024]{1,0:T(8,128)(2,1)} %get-tuple-element.29.refs_1_, ...), custom_call_target="tpu_custom_call" | custom-call | tf_op jit(solution)/shard_map/pallas_call | solution.py:999
  265.8 0.0 copy-start
  265.8 0.7 copy-done
  266.5 0.5 slice_bitcast_fusion.1
  267.0 0.1 constant_dynamic-slice_fusion
  267.0 0.5 slice_bitcast_fusion
  (5 shorter events, 0.1 us)
Async XLA Ops:
  2.0 0.7 copy-start.9
  2.0 0.7 copy-start.5
  2.0 0.7 copy-start.6
  2.0 0.7 copy-start.7
  2.0 0.7 copy-start.8
  2.0 0.7 copy-start.2
  2.1 0.7 copy-start.3
  2.1 0.7 copy-start.4
  2.9 0.7 copy-start.1
  265.8 0.7 copy-start

commit v3 on v2

--- a/solution.py
+++ b/solution.py
@@ -44,8 +44,9 @@
     return rate * (pulled - first - unit * second)
 
 
-SLOTS = 4
 LEAD = 1
+LOOK = 2
+RED_SPLIT = (0, 0, 0, 0)
 
 
 def scratch_list():
@@ -63,8 +64,7 @@
         win=v((6, 4, 2, 2, 64, 256), BF),
         wout=v((4, 2, 2, 2, 32, 1024), BF),
         wexp=v((4, 4, 2, 2, 64, 512), BF),
-        wred=v((4, 2, 2, 128, 1024), BF),
-        stage=v((2, 32, 2048), BF),
+        wred=v((4, 4, 4, 32, 1024), BF),
         qkv=v((3, 4, 768, 128), BF),
         mask=v((768, 768), BF),
         lse=v((4, 6, 8, 256), F32),
@@ -75,7 +75,7 @@
         middle=v((384, 1024), F32),
         out_acc=v((2, 384, 1024), F32),
         bn_acc=v((2, 384, 1024), F32),
-        cross=v((2, 384, 1024), F32),
+        cross=v((384, 1024), F32),
         ffb=v((3, 768, 512), BF),
         act_t=v((512, 768), BF),
         ba_all=v((2, 384, 512), BF),
@@ -83,13 +83,14 @@
         gvec=v((8, 1024), F32),
         gexp=v((4, 8, 512), F32),
         outx=v((4, 2, 2, 32, 1024), BF),
-        rb=v((SLOTS, 2, 4, 64, 512), BF),
-        ra=v((3, 4, 64, 512), BF),
-        rz=v((4, 3, 64, 512), BF),
+        rb=v((4, 2, 4, 64, 512), BF),
+        ra=v((4, 64, 512), BF),
+        rz=v((4, 6, 64, 512), BF),
+        rx=v((4, 2, 64, 512), BF),
+        ra_in=v((6, 4, 64, 256), BF),
         rz_in=v((6, 3, 64, 256), BF),
-        rb_red=v((SLOTS, 2, 128, 1024), BF),
-        ra_red=v((3, 128, 1024), BF),
-        rz_red=v((3, 128, 1024), BF),
+        rb_red=v((4, 2, 4, 32, 1024), BF),
+        land=v((4, 7, 32, 1024), BF),
         rb_out=v((2, 4, 32, 1024), BF),
         ra_out=v((4, 32, 1024), BF),
         rz_out=v((3, 32, 1024), BF),
@@ -108,6 +109,9 @@
         pre_r=dma((13,)),
         agz_s=dma((16, 3)),
         agz_r=dma((16, 3)),
+        agy_s=dma((16, 3)),
+        agy_r=dma((16, 3)),
+        agx_s=dma((16, 2)),
         aga_s=dma((16,)),
         aga_r=dma((16,)),
         agb_s=dma((16, 2)),
@@ -120,6 +124,10 @@
         rsa_r=dma((16,)),
         rsz_s=dma((16, 3)),
         rsz_r=dma((16, 3)),
+        rsy_s=dma((16, 3)),
+        rsy_r=dma((16, 3)),
+        rsx_s=dma((16, 2)),
+        rsx_r=dma((16, 2)),
         fin_s=dma((11,)),
         fin_r=dma((11,)),
     )
@@ -152,6 +160,12 @@
     z_dev = [(((z + k) % 4) * 4 + y * 2 + x, r) for k in (1, 2, 3)]
     z_at = [(z + k) % 4 for k in (1, 2, 3)]
     z_from = [(z + 4 - k) % 4 for k in (1, 2, 3)]
+    at_end = (z == 0) | (z == 3)
+    in_middle = (z == 1) | (z == 2)
+    far = z_from[1]
+    far_end = (jnp.where(z == 2, 3, 0) * 4 + y * 2 + x, r)
+    near_middle = (jnp.where(z == 0, 1, 2) * 4 + y * 2 + x, r)
+    place = 2 * y + x
 
     def copy(src, dst, ss, rs, dev):
         return pltpu.make_async_remote_copy(
@@ -169,11 +183,23 @@
     def part_cols(part, who):
         return pl.ds(pl.multiple_of((part // 2) * 1024 + who * 512 + (part % 2) * 256, 256), 256)
 
-    for block in range(16):
-        for who in range(2):
-            s.stage[who, :, block * 128 : (block + 1) * 128] = wexp_in[
-                :, (2 * block + who) * 128 : (2 * block + who + 1) * 128
+    group_32 = lax.broadcasted_iota(jnp.int32, (32, 128), 1) // 32
+
+    def pick(parts, group):
+        picked = parts[3]
+        for g in range(3):
+            picked = jnp.where(group == g, parts[g], picked)
+        return picked
+
+    for who in range(2):
+        for block in range(4):
+            source = [
+                wexp_in[:, (2 * (4 * block + q) + who) * 128 : (2 * (4 * block + q) + who + 1) * 128].astype(F32)
+                for q in range(4)
             ]
+            for j in range(4):
+                chosen = pick([source[(g + j) % 4] for g in range(4)], group_32)
+                s.half[who, j * 32 : (j + 1) * 32, block * 128 : (block + 1) * 128] = chosen.astype(BF)
     pre = []
     pre.append(copy(small_in, s.small.at[z, y, x, r], s.pre_s.at[0], s.pre_r.at[0], core_dev))
     for i in range(6):
@@ -190,7 +216,7 @@
     for j in range(4):
         pre.append(
             copy(
-                s.stage.at[o, :, pl.ds(j * 512, 512)],
+                s.half.at[o, j * 32 : (j + 1) * 32],
                 s.wexp.at[j, z, y, x, my_rows],
                 s.pre_s.at[8 + j],
                 s.pre_r.at[8 + j],
@@ -208,41 +234,85 @@
     for i in range(6):
         s.win[i, z, y, x, my_rows] = win_in[:, part_cols(i, r)]
     s.wout[z, y, x, r] = wout_in[...]
-    s.wred[z, y, x] = wred_in[...]
     for j in range(4):
-        s.wexp[j, z, y, x, my_rows] = s.stage[r, :, j * 512 : (j + 1) * 512]
-
-    def ag_small():
-        return Bag(t=0, piece=lambda a, b, c: s.small.at[a, b, c], col=lambda b, c: s.small.at[:, b, c], plane=None)
-
-    def ag_in(i):
-        return Bag(
-            t=1 + i, piece=lambda a, b, c: s.win.at[i, a, b, c], col=lambda b, c: s.win.at[i, :, b, c], plane=None
-        )
-
-    def ag_out():
-        return Bag(
-            t=7, piece=lambda a, b, c: s.wout.at[a, b, c, r], col=lambda b, c: s.wout.at[:, b, c, r], plane=None
-        )
-
-    def ag_exp(j):
-        return Bag(
-            t=8 + 2 * j,
-            piece=lambda a, b, c: s.wexp.at[j, a, b, c],
-            col=lambda b, c: s.wexp.at[j, :, b, c],
-            plane=None,
-        )
-
-    def ag_red(j):
-        return Bag(
-            t=9 + 2 * j, piece=lambda a, b, c: s.wred.at[j, b, c], col=lambda b, c: s.wred.at[j, b, c], plane=j
-        )
-
-    def z_copies(it):
-        return [
-            copy(it.piece(z, y, x), it.piece(z, y, x), s.agz_s.at[it.t, k], s.agz_r.at[it.t, k], z_dev[k])
-            for k in range(3)
-        ]
+        group = (place + 4 - j) % 4
+        s.wred[j, z, group] = wred_in[pl.ds(pl.multiple_of(group * 32, 32), 32)]
+    for j in range(4):
+        s.wexp[j, z, y, x, my_rows] = s.half[r, j * 32 : (j + 1) * 32]
+
+    def ag_item(t, piece, col, split):
+        return Bag(t=t, piece=piece, col=col, split=split)
+
+    def slot(j, b, c):
+        return (2 * b + c + 4 - j) % 4
+
+    gathers = [ag_item(0, lambda a, b, c: s.small.at[a, b, c], lambda b, c: s.small.at[:, b, c], False)]
+    for i in range(6):
+        gathers.append(
+            ag_item(
+                1 + i, lambda a, b, c, i=i: s.win.at[i, a, b, c], lambda b, c, i=i: s.win.at[i, :, b, c], False
+            )
+        )
+    gathers.append(ag_item(7, lambda a, b, c: s.wout.at[a, b, c, r], lambda b, c: s.wout.at[:, b, c, r], False))
+    for j in range(4):
+        gathers.append(
+            ag_item(
+                8 + 2 * j, lambda a, b, c, j=j: s.wexp.at[j, a, b, c], lambda b, c, j=j: s.wexp.at[j, :, b, c], True
+            )
+        )
+        gathers.append(
+            ag_item(
+                9 + 2 * j,
+                lambda a, b, c, j=j: s.wred.at[j, a, slot(j, b, c)],
+                lambda b, c, j=j: s.wred.at[j, :, slot(j, b, c)],
+                bool(RED_SPLIT[j]),
+            )
+        )
+
+    def when(cond, go):
+        if isinstance(cond, bool):
+            if cond:
+                go()
+        else:
+            pl.when(cond)(go)
+
+    def z_copies(it, yy, xx, ss, rs):
+        p = it.piece(z, yy, xx)
+        return [copy(p, p, ss.at[it.t, k], rs.at[it.t, k], z_dev[k]) for k in range(3)]
+
+    def straight(it, k):
+        if not it.split or k == 1:
+            return True
+        return z != 3 if k == 0 else z != 0
+
+    def z_start(it, yy, xx, ss, rs):
+        for k, c in enumerate(z_copies(it, yy, xx, ss, rs)):
+            when(straight(it, k), c.start)
+
+    def z_relay(it, yy, xx, rs, which):
+        p = it.piece(far, yy, xx)
+
+        @pl.when(in_middle)
+        def _():
+            copy(p, p, s.agx_s.at[it.t, which], rs.at[it.t, 1], far_end).wait_recv()
+            copy(p, p, s.agx_s.at[it.t, which], rs.at[it.t, jnp.where(z == 2, 2, 0)], far_end).start()
+
+    def z_wait(it, yy, xx, ss, rs):
+        for k in range(3):
+            p = it.piece(z_from[k], yy, xx)
+            c = copy(p, p, ss.at[it.t, k], rs.at[it.t, k], z_dev[k])
+            when(at_end if it.split and k == 1 else True, c.wait_recv)
+
+    def z_sent(it, yy, xx, ss, rs, which):
+        for k, c in enumerate(z_copies(it, yy, xx, ss, rs)):
+            when(straight(it, k), c.wait_send)
+        if it.split:
+            p = it.piece(far, yy, xx)
+            pl.when(in_middle)(copy(p, p, s.agx_s.at[it.t, which], rs.at[it.t, 0], far_end).wait_send)
+
+    def a_piece(it, yy, xx):
+        p = it.piece(z, yy, xx)
+        return copy(p, p, s.aga_s.at[it.t], s.aga_r.at[it.t], a_dev)
 
     def a_copy(it, yy, xx):
         return copy(it.col(yy, xx), it.col(yy, xx), s.aga_s.at[it.t], s.aga_r.at[it.t], a_dev)
@@ -251,32 +321,28 @@
         return copy(it.col(yy, xx), it.col(yy, xx), s.agb_s.at[it.t, which], s.agb_r.at[it.t, which], b_dev)
 
     def e0(it):
-        def go():
-            for c in z_copies(it):
-                c.start()
-
-        if it.plane is None:
-            go()
-        else:
-            pl.when(z == it.plane)(go)
+        if it.split:
+            a_piece(it, y, x).start()
+        z_start(it, y, x, s.agz_s, s.agz_r)
 
     def e1(it):
-        if it.plane is None:
-            for k in range(3):
-                p = it.piece(z_from[k], y, x)
-                copy(p, p, s.agz_s.at[it.t, k], s.agz_r.at[it.t, k], z_dev[k]).wait_recv()
-        else:
-
-            @pl.when(z != it.plane)
-            def _():
-                k = (z + 4 - it.plane) % 4 - 1
-                p = it.piece(z, y, x)
-                copy(p, p, s.agz_s.at[it.t, k], s.agz_r.at[it.t, k], z_dev[0]).wait_recv()
-
+        if it.split:
+            z_relay(it, y, x, s.agz_r, 0)
+            a_piece(it, ya, xa).wait_recv()
+            z_start(it, ya, xa, s.agy_s, s.agy_r)
+            return
+        z_wait(it, y, x, s.agz_s, s.agz_r)
         a_copy(it, y, x).start()
         b_copy(it, 0, y, x).start()
 
     def e2(it):
+        if it.split:
+            z_relay(it, ya, xa, s.agy_r, 1)
+            z_wait(it, y, x, s.agz_s, s.agz_r)
+            b_copy(it, 0, y, x).start()
+            z_wait(it, ya, xa, s.agy_s, s.agy_r)
+            b_copy(it, 1, ya, xa).start()
+            return
         a_copy(it, ya, xa).wait_recv()
         b_copy(it, 1, ya, xa).start()
 
@@ -285,35 +351,46 @@
         b_copy(it, 1, yc, xc).wait_recv()
 
     def sent(it):
-        def go():
-            for c in z_copies(it):
-                c.wait_send()
-
-        if it.plane is None:
-            go()
+        z_sent(it, y, x, s.agz_s, s.agz_r, 0)
+        if it.split:
+            a_piece(it, y, x).wait_send()
+            z_sent(it, ya, xa, s.agy_s, s.agy_r, 1)
         else:
-            pl.when(z == it.plane)(go)
-        a_copy(it, y, x).wait_send()
+            a_copy(it, y, x).wait_send()
         b_copy(it, 0, y, x).wait_send()
         b_copy(it, 1, ya, xa).wait_send()
 
-    i_small, i_out = ag_small(), ag_out()
-    i_w = [ag_in(i) for i in range(6)]
-
     def pre_in(index, dst):
         copy(dst, dst, s.pre_s.at[index], s.pre_r.at[index], core_dev).wait_recv()
 
-    def begin(i):
-        pre_in(1 + i, s.win.at[i, z, y, x, o_rows])
-        e0(i_w[i])
-
-    pre_in(0, s.small.at[z, y, x, o])
-    e0(i_small)
-    begin(0)
-    begin(1)
-    e1(i_small)
-    e1(i_w[0])
-    begin(2)
+    def ready(i):
+        if i == 0:
+            pre_in(0, s.small.at[z, y, x, o])
+        elif i < 7:
+            pre_in(i, s.win.at[i - 1, z, y, x, o_rows])
+        elif i >= 8 and i % 2 == 0:
+            j = (i - 8) // 2
+            pre_in(8 + j, s.wexp.at[j, z, y, x, o_rows])
+
+    def gather(i):
+        for event, lag in ((e0, 0), (e1, LOOK), (e2, 2 * LOOK), (e3, 3 * LOOK)):
+            if 0 <= i - lag < len(gathers):
+                if lag == 0:
+                    ready(i)
+                event(gathers[i - lag])
+
+    for i in range(3):
+        gather(i)
+
+    for edge, k in ((0, 0), (3, 2)):
+
+        @pl.when(z == edge)
+        def _(k=k):
+            for base in (0, 3):
+                s.rz[:, base + k] = jnp.zeros((4, 64, 512), BF)
+                for j in range(4):
+                    if RED_SPLIT[j]:
+                        s.land[j, 1 + base + k] = jnp.zeros((32, 1024), BF)
 
     own_frames.wait()
     own_cot.wait()
@@ -333,11 +410,8 @@
     s.mask[0:384, 384:768] = as_bias(seen)
     s.mask[384:768, 384:768] = as_bias(causal & (seg_wide == seg_tall))
 
-    e2(i_small)
-    e1(i_w[1])
-    e2(i_w[0])
-    begin(3)
-    e3(i_small)
+    for i in range(3, 3 * LOOK + 1):
+        gather(i)
 
     def tile_sum(q):
         total = jnp.zeros((16, 128), F32)
@@ -348,11 +422,11 @@
 
     for q in range(8):
         s.vec[:, q * 128 : (q + 1) * 128] = tile_sum(q)[0:8]
-    for j in range(4):
-        for yy in range(2):
-            for xx in range(2):
-                at = (yy * 2 + xx) * 128
-                s.ebias[j, 0:1, at : at + 128] = s.small[j, yy, xx, r].astype(F32)[8:9]
+    group_1 = lax.broadcasted_iota(jnp.int32, (1, 128), 1) // 32
+    for block in range(4):
+        tiles = [s.small[block, q // 2, q % 2, r].astype(F32)[8:9] for q in range(4)]
+        for j in range(4):
+            s.ebias[j, 0:1, block * 128 : (block + 1) * 128] = pick([tiles[(g + j) % 4] for g in range(4)], group_1)
 
     def vec_row(i):
         return s.vec[i : i + 1, :]
@@ -380,39 +454,9 @@
         s.qkv[section, 2 * n] = mixed[:, 0:128]
         s.qkv[section, 2 * n + 1] = mixed[:, 128:256]
 
-    e1(i_w[2])
-    e2(i_w[1])
-    begin(4)
-    e3(i_w[0])
-    project(0)
-    e1(i_w[3])
-    e2(i_w[2])
-    begin(5)
-    e3(i_w[1])
-    project(1)
-    e1(i_w[4])
-    e2(i_w[3])
-    e0(i_out)
-    e3(i_w[2])
-    project(2)
-    for j in range(4):
-        pre_in(8 + j, s.wexp.at[j, z, y, x, o_rows])
-    e1(i_w[5])
-    e2(i_w[4])
-    e0(ag_exp(0))
-    e3(i_w[3])
-    project(3)
-    e1(i_out)
-    e2(i_w[5])
-    e0(ag_red(0))
-    e3(i_w[4])
-    project(4)
-    e1(ag_exp(0))
-    e2(i_out)
-    e3(i_w[5])
-    project(5)
-    e0(ag_exp(1))
-    e1(ag_red(0))
+    for part in range(6):
+        gather(3 * LOOK + 1 + part)
+        project(part)
 
     factor = HD**-0.5 * LOG2E
     low_lane = lax.broadcasted_iota(jnp.int32, (128, 128), 1) < 64
@@ -446,6 +490,8 @@
             s.half[rb // 3, at : at + 128, dims] = out.T.astype(BF)
         return carry
 
+    for j in range(4):
+        pre[8 + j].wait_send()
     lax.fori_loop(0, 4, attend, 0)
 
     my_half = pl.ds(pl.multiple_of(r * 512, 512), 512)
@@ -458,17 +504,12 @@
     core_copy(1, s.half_t.at[o], s.att_t.at[my_half]).start()
     s.wide[:, my_half] = s.half[r]
     s.att_t[my_half] = s.half_t[r]
-    e2(ag_exp(0))
-    e3(i_out)
+    gather(3 * LOOK + 7)
     out_swap = core_copy(2, s.wout.at[:, :, :, r], s.wout.at[:, :, :, r])
     out_swap.start()
     core_copy(0, s.wide.at[:, o_half], s.wide.at[:, o_half]).wait_recv()
     core_copy(1, s.att_t.at[o_half], s.att_t.at[o_half]).wait_recv()
     core_copy(2, s.wout.at[:, :, :, o], s.wout.at[:, :, :, o]).wait_recv()
-    e0(ag_red(1))
-    e1(ag_exp(1))
-    e2(ag_red(0))
-
     def out_tile(n, carry):
         cols = pl.ds(pl.multiple_of(n * 256, 256), 256)
         branch = dot(s.wide[...], s.wout[:, :, :, :, :, cols].reshape(1024, 256))
@@ -489,6 +530,7 @@
     s.out_acc[...] = jnp.zeros_like(s.out_acc)
     s.bn_acc[...] = jnp.zeros_like(s.bn_acc)
     core_copy(3, s.n_all.at[o], s.n_all.at[o]).wait_recv()
+    core_copy(3, s.n_all.at[r], s.n_all.at[r]).wait_send()
 
     def flip_two(i, carry):
         who, rows = i // 3, pl.ds(pl.multiple_of((i % 3) * 128, 128), 128)
@@ -499,38 +541,39 @@
 
     def rs_exp(j):
         return Bag(
-            t=j, fin=j, parts=4, plane=None, piece=lambda a, b, c: s.wexp.at[j, a, b, c],
-            col=lambda b, c: s.wexp.at[j, :, b, c], rb=lambda w: s.rb.at[j % SLOTS, w], ra=s.ra.at[j % 3],
-            rz=lambda k: s.rz.at[j, k],
+            t=j, fin=j, split=True, piece=lambda a, b, c: s.wexp.at[j, a, b, c],
+            col=lambda b, c: s.wexp.at[j, :, b, c], rb=lambda w: s.rb.at[j, w], ra=s.ra.at[j],
+            rz=lambda k: s.rz.at[j, k], rx=lambda w: s.rx.at[j, w],
         )
 
     def rs_in(i):
         slot, part = ((0, 0), (1, 0), (0, 1), (1, 1), (2, 0), (2, 1))[i]
         half = slice(256 * part, 256 * part + 256)
-        again = slice(256 * (i % 2), 256 * (i % 2) + 256)
         return Bag(
-            t=9 + i, fin=4 + i, parts=4, plane=None, piece=lambda a, b, c: s.win.at[i, a, b, c],
+            t=9 + i, fin=4 + i, split=False, piece=lambda a, b, c: s.win.at[i, a, b, c],
             col=lambda b, c: s.win.at[i, :, b, c], rb=lambda w: s.rb.at[slot, w, :, :, half],
-            ra=s.ra.at[(1, 2, 0)[i // 2], :, :, again], rz=lambda k: s.rz_in.at[i, k],
+            ra=s.ra_in.at[i], rz=lambda k: s.rz_in.at[i, k],
         )
 
     def rs_red(j):
+        split = bool(RED_SPLIT[j])
         return Bag(
-            t=4 + j, fin=None, parts=1, plane=j, piece=lambda a, b, c: s.wred.at[j, b, c],
-            col=lambda b, c: s.wred.at[j, b, c], rb=lambda w: s.rb_red.at[j % SLOTS, w],
-            ra=s.ra_red.at[j % 3], rz=lambda k: s.rz_red.at[k],
+            t=4 + j, fin=None, split=split, piece=lambda a, b, c: s.wred.at[j, a, slot(j, b, c)],
+            col=lambda b, c: s.wred.at[j, :, slot(j, b, c)], rb=lambda w: s.rb_red.at[j, w],
+            ra=s.land.at[j, 0] if split else s.land.at[j, 0:4],
+            rz=lambda k: s.land.at[j, k + (1 if split else 4)], rx=lambda w: s.land.at[j, 7 + w],
         )
 
     def rs_out():
         return Bag(
-            t=8, fin=None, parts=4, plane=None, piece=lambda a, b, c: s.wout.at[a, b, c, r],
+            t=8, fin=None, split=False, piece=lambda a, b, c: s.wout.at[a, b, c, r],
             col=lambda b, c: s.wout.at[:, b, c, r], rb=lambda w: s.rb_out.at[w], ra=s.ra_out,
             rz=lambda k: s.rz_out.at[k],
         )
 
     def rs_small():
         return Bag(
-            t=15, fin=None, parts=4, plane=None, piece=lambda a, b, c: s.sg.at[a, b, c],
+            t=15, fin=None, split=False, piece=lambda a, b, c: s.sg.at[a, b, c],
             col=lambda b, c: s.sg.at[:, b, c], rb=lambda w: s.rb_sg.at[w], ra=s.ra_sg,
             rz=lambda k: s.rz_sg.at[k],
         )
@@ -539,33 +582,80 @@
         return copy(it.col(yy, xx), it.rb(which), s.rsb_s.at[it.t, which], s.rsb_r.at[it.t, which], b_dev)
 
     def ra_copy(it):
-        return copy(it.col(ya, xa), it.ra, s.rsa_s.at[it.t], s.rsa_r.at[it.t], a_dev)
-
-    def rz_copy(it, k, at):
-        return copy(it.piece(at, y, x), it.rz(k), s.rsz_s.at[it.t, k], s.rsz_r.at[it.t, k], z_dev[k])
+        src = it.piece(z, ya, xa) if it.split else it.col(ya, xa)
+        return copy(src, it.ra, s.rsa_s.at[it.t], s.rsa_r.at[it.t], a_dev)
 
     def add_into(it, yy, xx, sources):
         target = it.col(yy, xx)
         kind = F32 if it.t == 15 else BF
 
-        def one(at):
-            total = target[at].astype(F32)
+        def body(i, carry):
+            total = target[i].astype(F32)
             for src in sources:
-                total = total + src[at].astype(F32)
-            target[at] = total.astype(kind)
-
-        if it.parts == 4:
-
-            def body(i, carry):
-                one(i)
-                return carry
-        else:
-
-            def body(i, carry):
-                one(pl.ds(pl.multiple_of(i * 32, 32), 32))
-                return carry
+                total = total + src[i].astype(F32)
+            target[i] = total.astype(kind)
+            return carry
 
         lax.fori_loop(0, 4, body, 0)
+
+    def own_copy(it, k, yy, xx, base, ss, rs):
+        return copy(it.piece(z_at[k], yy, xx), it.rz(base + k), ss.at[it.t, k], rs.at[it.t, k], z_dev[k])
+
+    def far_copy(it, k, yy, xx, which):
+        return copy(
+            it.piece(z_at[k], yy, xx), it.rx(which), s.rsx_s.at[it.t, which], s.rsx_r.at[it.t, which], near_middle
+        )
+
+    def own_start(it, yy, xx, base, ss, rs, which):
+        for k in range(3):
+            c = own_copy(it, k, yy, xx, base, ss, rs)
+            if not it.split:
+                c.start()
+            elif k == 1:
+                pl.when(at_end)(c.start)
+            else:
+                edge = 3 if k == 0 else 0
+                pl.when(z != edge)(c.start)
+                pl.when(z == edge)(far_copy(it, k, yy, xx, which).start)
+
+    def own_relay(it, yy, xx, base, ss, rs, which):
+        @pl.when(in_middle)
+        def _():
+            far_copy(it, 1, yy, xx, which).wait_recv()
+            held = it.piece(z_at[1], yy, xx)
+            held[...] = (held[...].astype(F32) + it.rx(which)[...].astype(F32)).astype(BF)
+            own_copy(it, 1, yy, xx, base, ss, rs).start()
+
+    def own_wait(it, yy, xx, base, ss, rs):
+        for k in range(3):
+            c = own_copy(it, k, yy, xx, base, ss, rs)
+            if not it.split or k == 1:
+                c.wait_recv()
+            else:
+                pl.when(z != (0 if k == 0 else 3))(c.wait_recv)
+
+    def own_sent(it, yy, xx, base, ss, rs, which):
+        for k in range(3):
+            c = own_copy(it, k, yy, xx, base, ss, rs)
+            if not it.split or k == 1:
+                c.wait_send()
+            else:
+                edge = 3 if k == 0 else 0
+                pl.when(z != edge)(c.wait_send)
+                pl.when(z == edge)(far_copy(it, k, yy, xx, which).wait_send)
+
+    def z_args(it, second):
+        if second:
+            return (ya, xa, 3, s.rsy_s, s.rsy_r)
+        return (y, x, 0, s.rsz_s, s.rsz_r)
+
+    def z_total(it, second):
+        yy, xx, base, ss, rs = z_args(it, second)
+        own_wait(it, yy, xx, base, ss, rs)
+        total = it.piece(z, yy, xx)[...].astype(F32)
+        for k in range(3):
+            total = total + it.rz(base + k)[...].astype(F32)
+        return total
 
     def f0(it):
         rb_copy(it, 0, yc, xc).start()
@@ -574,32 +664,35 @@
     def f1(it):
         rb_copy(it, 0, yc, xc).wait_recv()
         add_into(it, ya, xa, [it.rb(0)])
-        ra_copy(it).start()
+        if not it.split:
+            ra_copy(it).start()
+            return
+        own_start(it, *z_args(it, True), 1)
+        rb_copy(it, 1, yb, xb).wait_recv()
+        add_into(it, y, x, [it.rb(1)])
+        own_start(it, *z_args(it, False), 0)
 
     def f2(it):
+        if it.split:
+            own_relay(it, *z_args(it, True), 1)
+            own_relay(it, *z_args(it, False), 0)
+            return
         rb_copy(it, 1, yb, xb).wait_recv()
         ra_copy(it).wait_recv()
         add_into(it, y, x, [it.rb(1), it.ra])
-
-        if it.plane is None:
-            for k in range(3):
-                rz_copy(it, k, z_at[k]).start()
-        else:
-
-            @pl.when(z != it.plane)
-            def _():
-                k = (it.plane + 4 - z) % 4 - 1
-                copy(
-                    it.piece(z, y, x), it.rz(k), s.rsz_s.at[it.t, k], s.rsz_r.at[it.t, k],
-                    (it.plane * 4 + y * 2 + x, r),
-                ).start()
-
-    def z_total(it):
-        for k in range(3):
-            rz_copy(it, k, z_at[k]).wait_recv()
-        total = it.piece(z, y, x)[...].astype(F32)
-        for k in range(3):
-            total = total + it.rz(k)[...].astype(F32)
+        own_start(it, *z_args(it, False), 0)
+
+    def f3(it):
+        if it.split:
+            total = z_total(it, True)
+            it.piece(z, ya, xa)[...] = total.astype(BF)
+            ra_copy(it).start()
+
+    def full_total(it):
+        total = z_total(it, False)
+        if it.split:
+            ra_copy(it).wait_recv()
+            total = total + it.ra[...].astype(F32)
         return total
 
     def fin_refs(index):
@@ -614,35 +707,41 @@
     def small_fin():
         return copy(s.sfin, s.sfin_in, s.fin_s.at[10], s.fin_r.at[10], core_dev)
 
-    def put(index, value, who):
-        if index < 4:
-            for i in range(4):
-                at = pl.ds(pl.multiple_of((2 * (4 * index + i) + who) * 128, 128), 128)
-                dwexp_ref[:, at] = value[:, i * 128 : (i + 1) * 128]
-        else:
-            dwin_ref[:, part_cols(index - 4, who)] = value
+    def put_in(i, value, who):
+        dwin_ref[:, part_cols(i, who)] = value
+
+    def put_exp(source, who):
+        for block in range(4):
+            at = slice(block * 128, (block + 1) * 128)
+            chunk = [source(j)[:, at] for j in range(4)]
+            for q in range(4):
+                cols = pl.ds(pl.multiple_of((2 * (4 * block + q) + who) * 128, 128), 128)
+                dwexp_ref[:, cols] = pick([chunk[(q - g) % 4] for g in range(4)], group_32)
 
     def f4(it):
-        if it.plane is not None:
-
-            @pl.when(z == it.plane)
-            def _():
-                dwred_ref[...] = z_total(it)
+        if 4 <= it.t < 8:
+            group = (place + 8 - it.t) % 4
+            dwred_ref[pl.ds(pl.multiple_of(group * 32, 32), 32)] = full_total(it)
         elif it.t == 8:
-            dwout_ref[...] = z_total(it)
+            dwout_ref[...] = full_total(it)
         elif it.t == 15:
-            s.sfin[...] = z_total(it)
+            s.sfin[...] = full_total(it)
             small_fin().start()
         else:
             out, _ = fin_refs(it.fin)
-            out[...] = z_total(it)
+            out[...] = full_total(it)
             fin_copy(it.fin).start()
-            put(it.fin, out[my_rows], r)
+            if it.fin >= 4:
+                put_in(it.fin - 4, out[my_rows], r)
 
     def f5(it):
         if it.fin is not None:
             fin_copy(it.fin).wait_recv()
-            put(it.fin, fin_refs(it.fin)[1][...], o)
+            if it.fin >= 4:
+                put_in(it.fin - 4, fin_refs(it.fin)[1][...], o)
+            elif it.fin == 3:
+                put_exp(lambda j: s.fin[j, my_rows], r)
+                put_exp(lambda j: s.fin_in[j], o)
         elif it.t == 15:
             small_fin().wait_recv()
             row = lax.broadcasted_iota(jnp.int32, (16, 128), 0)
@@ -653,18 +752,9 @@
         rb_copy(it, 0, yc, xc).wait_send()
         rb_copy(it, 1, yb, xb).wait_send()
         ra_copy(it).wait_send()
-        if it.plane is None:
-            for k in range(3):
-                rz_copy(it, k, z_at[k]).wait_send()
-        else:
-
-            @pl.when(z != it.plane)
-            def _():
-                k = (it.plane + 4 - z) % 4 - 1
-                copy(
-                    it.piece(z, y, x), it.rz(k), s.rsz_s.at[it.t, k], s.rsz_r.at[it.t, k],
-                    (it.plane * 4 + y * 2 + x, r),
-                ).wait_send()
+        own_sent(it, *z_args(it, False), 0)
+        if it.split:
+            own_sent(it, *z_args(it, True), 1)
         if it.fin is not None:
             fin_copy(it.fin).wait_send()
         elif it.t == 15:
@@ -676,34 +766,15 @@
     order += [rs_out()] + [rs_in(i) for i in range(6)] + [rs_small()]
 
     def step(i):
-        for event, lag in ((f0, -LEAD), (f1, 1), (f2, 2), (f4, 3), (f5, 4)):
+        for event, lag in ((f0, -LEAD), (f1, 1), (f2, 2), (f3, 3), (f4, 4), (f5, 5)):
             if 0 <= i - lag < len(order):
                 event(order[i - lag])
 
-    def when(cond, go):
-        if isinstance(cond, bool):
-            if cond:
-                go()
-        else:
-            pl.when(cond)(go)
-
     def feed(j, between):
-        def ahead_one():
-            e1(ag_red(j + 1))
-            e2(ag_exp(j + 1))
-
-        def ahead_two():
-            e0(ag_red(j + 2))
-            e1(ag_exp(j + 2))
-
-        when(j < 2, lambda: e0(ag_exp(j + 2)))
-        when(j < 3, ahead_one)
-        e3(ag_exp(j))
-        when(j < 2, ahead_two)
-        when(j < 3, lambda: e2(ag_red(j + 1)))
-        e3(ag_red(j))
-        sent(ag_exp(j))
-        sent(ag_red(j))
+        gather(3 * LOOK + 8 + 2 * j)
+        gather(3 * LOOK + 9 + 2 * j)
+        sent(gathers[8 + 2 * j])
+        sent(gathers[9 + 2 * j])
         between(0)
 
         def hidden(n, inside):
@@ -716,7 +787,8 @@
             s.act_t[cols] = active.T.astype(BF)
             slope = phi + inner * (jnp.exp(-0.5 * inner * inner) * 0.3989422804014327)
             up = s.c_all[...].reshape(768, 1024)
-            back = (dot_nt(up, s.wred[j, n].reshape(256, 1024)) * slope).astype(BF)
+            weight = s.wred[j, pl.ds(2 * n, 2)].reshape(256, 1024)
+            back = (dot_nt(up, weight) * slope).astype(BF)
             s.ffb[1, :, cols] = back
             s.gexp[j, 0:1, cols] = jnp.sum(back.astype(F32), axis=0, keepdims=True)
             return inside
@@ -737,7 +809,7 @@
         def grad_red(n, inside):
             cols = pl.ds(pl.multiple_of(n * 256, 256), 256)
             up = s.c_all[:, :, cols].reshape(768, 256)
-            s.wred[j, :, :, :, cols] = dot(s.act_t[...], up).astype(BF).reshape(2, 2, 128, 256)
+            s.wred[j, :, :, :, cols] = dot(s.act_t[...], up).astype(BF).reshape(4, 4, 32, 256)
             return inside
 
         lax.fori_loop(0, 4, grad_red, 0)
@@ -751,32 +823,30 @@
         lax.fori_loop(0, 2, grad_exp, 0)
         between(2)
 
-    def early_feed(j, carry):
+    for j in range(3):
         feed(j, lambda place: None)
-        return carry
-
-    lax.fori_loop(0, 3, early_feed, 0)
-
-    def start_reduction(place):
-        if place == 0:
+
+    def start_reduction(place_in):
+        if place_in == 0:
             for it in order[:LEAD]:
                 f0(it)
             step(0)
-        elif place == 1:
-            core_copy(4, s.bn_acc.at[o], s.cross.at[0]).start()
-            core_copy(5, s.out_acc.at[o], s.cross.at[1]).start()
+        elif place_in == 1:
+            core_copy(4, s.bn_acc.at[o], s.cross).start()
             step(1)
         else:
             step(2)
 
     feed(3, start_reduction)
 
-    core_copy(4, s.bn_acc.at[o], s.cross.at[0]).wait_recv()
+    core_copy(4, s.bn_acc.at[o], s.cross).wait_recv()
+    s.n_all[o] = s.out_acc[o].astype(BF)
+    core_copy(5, s.n_all.at[o], s.n_all.at[o]).start()
 
     def middle_back(i, carry):
         rows = pl.ds(pl.multiple_of(i * 128, 128), 128)
         unit, rate = centre(s.middle[rows])
-        upstream = s.bn_acc[r, rows] + s.cross[0, rows]
+        upstream = s.bn_acc[r, rows] + s.cross[rows]
         cot = s.c_all[r, rows].astype(F32)
         back = cot + norm_back(unit, rate, vec_row(5), upstream)
         s.bn_acc[r, rows] = back
@@ -810,7 +880,7 @@
     core_copy(6, s.half.at[o], s.ba_all.at[r]).start()
     s.ba_all[r] = s.half[r]
     step(3)
-    sent(i_out)
+    sent(gathers[7])
 
     def grad_out(n, carry):
         cols = pl.ds(pl.multiple_of(n * 256, 256), 256)
@@ -820,11 +890,11 @@
 
     lax.fori_loop(0, 4, grad_out, 0)
     core_copy(7, s.wout.at[:, :, :, o], s.outx).start()
-    core_copy(5, s.out_acc.at[o], s.cross.at[1]).wait_recv()
+    core_copy(5, s.n_all.at[r], s.n_all.at[r]).wait_recv()
 
     def result_tile(i, carry):
         rows = pl.ds(pl.multiple_of(i * 128, 128), 128)
-        total = s.middle[rows] + s.out_acc[r, rows] + s.cross[1, rows] + vec_row(7)
+        total = s.middle[rows] + s.out_acc[r, rows] + s.n_all[r, rows].astype(F32) + vec_row(7)
         result_ref[rows] = total.astype(BF)
         return carry
 
@@ -873,7 +943,7 @@
     step(5)
     lax.fori_loop(3, 4, attend_back, 0)
 
-    core_copy(5, s.out_acc.at[o], s.cross.at[1]).wait_send()
+    core_copy(5, s.n_all.at[o], s.n_all.at[o]).wait_send()
 
     def back_in(n, carry):
         cols = pl.ds(pl.multiple_of(n * 256, 256), 256)
@@ -885,10 +955,10 @@
         return carry
 
     lax.fori_loop(0, 4, back_in, 0)
-    core_copy(8, s.out_acc.at[o], s.cross.at[0]).start()
+    core_copy(8, s.out_acc.at[o], s.cross).start()
     step(6)
     for part in range(6):
-        sent(i_w[part])
+        sent(gathers[1 + part])
         at = (part % 2) * 256
         grad = dot(s.n1t[...], s.ffb[part // 2, :, at : at + 256]).astype(BF)
         s.win[part] = grad.reshape(4, 2, 2, 64, 256)
@@ -897,12 +967,12 @@
     step(8)
     step(9)
 
-    core_copy(8, s.out_acc.at[o], s.cross.at[0]).wait_recv()
+    core_copy(8, s.out_acc.at[o], s.cross).wait_recv()
 
     def frame_back(i, carry):
         rows = pl.ds(pl.multiple_of(i * 128, 128), 128)
         unit, rate = centre(s.frames_all[r, rows].astype(F32))
-        upstream = s.out_acc[r, rows] + s.cross[0, rows]
+        upstream = s.out_acc[r, rows] + s.cross[rows]
         back = s.bn_acc[r, rows] + norm_back(unit, rate, vec_row(0), upstream)
         fgrad_ref[rows] = back.astype(BF)
         gain_t, shift_t = carry
@@ -923,21 +993,23 @@
             for xx in range(2):
                 at = (zz * 2 + yy) * 128
                 s.sg[zz, yy, xx, 0:8] = s.gvec[:, at : at + 128]
-                at = (yy * 2 + xx) * 128
-                s.sg[zz, yy, xx, 8:9] = s.gexp[zz, 0:1, at : at + 128]
-
-    for i in range(10, len(order) + 4):
+                q = 2 * yy + xx
+                block = slice(zz * 128, (zz + 1) * 128)
+                chunk = [s.gexp[j, 0:1, block] for j in range(4)]
+                s.sg[zz, yy, xx, 8:9] = pick([chunk[(q - g) % 4] for g in range(4)], group_1)
+
+    for i in range(10, len(order) + 5):
         step(i)
 
-    for item in pre:
-        item.wait_send()
-    sent(i_small)
+    for i, item in enumerate(pre):
+        if not 8 <= i < 12:
+            item.wait_send()
+    sent(gathers[0])
     core_copy(1, s.half_t.at[o], s.half_t.at[o]).wait_send()
-    core_copy(3, s.n_all.at[r], s.n_all.at[r]).wait_send()
-    core_copy(4, s.bn_acc.at[o], s.cross.at[0]).wait_send()
+    core_copy(4, s.bn_acc.at[o], s.cross).wait_send()
     core_copy(6, s.half.at[o], s.ba_all.at[r]).wait_send()
     core_copy(7, s.wout.at[:, :, :, o], s.outx).wait_send()
-    core_copy(8, s.out_acc.at[o], s.cross.at[0]).wait_send()
+    core_copy(8, s.out_acc.at[o], s.cross).wait_send()
     for it in order:
         all_sent(it)
 

time: 268 us -> 243 us (0.907)
  Pallas kernels: 262 us -> 236 us
    pallas_call x1, Pallas kernels: 259 us -> 234 us  [fused_shards(): pl.pallas_call(functools.partial(layer_kernel, tuple(scratch)), out_shape...]
where the time goes in v3:
time: 243 us; the launch traced here: 242 us
  Pallas kernels  236 us (97%)
  local copies, waits for them, and re-layouts  3.29 us (1%)
    pallas_call x1, Pallas kernels, fused_shards(): pl.pallas_call(functools.partial(layer_kernel, tuple(scratch)), out_shape...  234 us

profile of v3, /device:TPU:1, one launch (start us, length us, event | category | flops | bytes accessed | tf_op | source)
XLA Modules:
  0.0 242.5 jit_solution(2900298201055090481)
XLA Ops:
  2.0 0.0 copy-start.9
  2.0 0.0 copy-start.5
  2.0 0.0 copy-start.6
  2.0 0.0 copy-start.7
  2.0 0.0 copy-start.8
  2.0 0.0 copy-start.2
  2.1 0.0 copy-start.3
  2.1 0.0 copy-start.4
  2.1 0.1 pad.2.clone
  2.2 0.5 copy-done.9
  2.6 0.0 copy-done.5
  2.6 0.0 copy-done.6
  2.7 0.0 copy-done.7
  2.7 0.0 copy-done.8
  2.7 0.0 copy-done.2
  2.7 0.0 copy-done.3
  2.7 0.0 copy-done.4
  2.8 0.1 tile.10
  2.9 0.0 copy-start.1
  2.9 0.6 copy-done.1
  3.5 0.7 maximum_maximum_fusion.refs_5_
  4.2 233.5 %shard_map.289 = (bf16[384,1024]{1,0:T(8,128)(2,1)}, bf16[384,1024]{1,0:T(8,128)(2,1)}, f32[32,3072]{1,0:T(8,128)}, f32[32,1024]{1,0:T(8,128)}, f32[32,4096]{1,0...) custom-call(s32[1]{0:T(128)S(6)} %copy.33.refs_0_, s32[1]{0:T(128)S(6)} %copy.34.refs_1_, s32[1,384]{1,0:T(1,128)} %refs_2_.1, ...), custom_call_target="tpu_custom_call" | custom-call | tf_op jit(solution)/shard_map/pallas_call | solution.py:1049
  237.7 2.9 %shard_map.290 = (bf16[384,1024]{1,0:T(8,128)(2,1)}, bf16[384,1024]{1,0:T(8,128)(2,1)}, f32[32,3072]{1,0:T(8,128)}, f32[32,1024]{1,0:T(8,128)}, f32[32,4096]{1,0:T(8,128)}, /*index=5*/f32[128,1024]{1,0:T(8,128)}) custom-call(bf16[384,1024]{1,0:T(8,128)(2,1)} %get-tuple-element.28.refs_0_, bf16[384,1024]{1,0:T(8,128)(2,1)} %get-tuple-element.29.refs_1_, ...), custom_call_target="tpu_custom_call" | custom-call | tf_op jit(solution)/shard_map/pallas_call | solution.py:1071
  240.6 0.0 copy-start
  240.6 0.7 copy-done
  241.3 0.5 slice_bitcast_fusion.1
  241.8 0.1 constant_dynamic-slice_fusion
  241.9 0.5 slice_bitcast_fusion
  (5 shorter events, 0.1 us)
Async XLA Ops:
  2.0 0.7 copy-start.9
  2.0 0.7 copy-start.5
  2.0 0.7 copy-start.6
  2.0 0.7 copy-start.7
  2.0 0.7 copy-start.8
  2.0 0.7 copy-start.2
  2.1 0.7 copy-start.3
  2.1 0.7 copy-start.4
  2.9 0.7 copy-start.1
  240.6 0.7 copy-start

commit v4 on v3

--- a/solution.py
+++ b/solution.py
@@ -45,7 +45,10 @@
 
 
 LEAD = 1
+EARLY_CHUNK = 2
 LOOK = 2
+LAG_IN = 7
+LAG_FF = 7
 RED_SPLIT = (0, 0, 0, 0)
 
 
@@ -183,23 +186,6 @@
     def part_cols(part, who):
         return pl.ds(pl.multiple_of((part // 2) * 1024 + who * 512 + (part % 2) * 256, 256), 256)
 
-    group_32 = lax.broadcasted_iota(jnp.int32, (32, 128), 1) // 32
-
-    def pick(parts, group):
-        picked = parts[3]
-        for g in range(3):
-            picked = jnp.where(group == g, parts[g], picked)
-        return picked
-
-    for who in range(2):
-        for block in range(4):
-            source = [
-                wexp_in[:, (2 * (4 * block + q) + who) * 128 : (2 * (4 * block + q) + who + 1) * 128].astype(F32)
-                for q in range(4)
-            ]
-            for j in range(4):
-                chosen = pick([source[(g + j) % 4] for g in range(4)], group_32)
-                s.half[who, j * 32 : (j + 1) * 32, block * 128 : (block + 1) * 128] = chosen.astype(BF)
     pre = []
     pre.append(copy(small_in, s.small.at[z, y, x, r], s.pre_s.at[0], s.pre_r.at[0], core_dev))
     for i in range(6):
@@ -224,7 +210,26 @@
             )
         )
     pre.append(copy(cot_ref, s.c_all.at[r], s.pre_s.at[12], s.pre_r.at[12], core_dev))
-    for item in pre:
+    for item in pre[:8]:
+        item.start()
+    group_32 = lax.broadcasted_iota(jnp.int32, (32, 128), 1) // 32
+
+    def pick(parts, group):
+        picked = parts[3]
+        for g in range(3):
+            picked = jnp.where(group == g, parts[g], picked)
+        return picked
+
+    for who in range(2):
+        for block in range(4):
+            source = [
+                wexp_in[:, (2 * (4 * block + q) + who) * 128 : (2 * (4 * block + q) + who + 1) * 128].astype(F32)
+                for q in range(4)
+            ]
+            for j in range(4):
+                chosen = pick([source[(g + j) % 4] for g in range(4)], group_32)
+                s.half[who, j * 32 : (j + 1) * 32, block * 128 : (block + 1) * 128] = chosen.astype(BF)
+    for item in pre[8:]:
         item.start()
     own_frames = pltpu.make_async_copy(frames_ref, s.frames_all.at[r], s.own_s.at[0])
     own_cot = pltpu.make_async_copy(cot_ref, s.c_all.at[r], s.own_s.at[1])
@@ -372,15 +377,22 @@
             j = (i - 8) // 2
             pre_in(8 + j, s.wexp.at[j, z, y, x, o_rows])
 
-    def gather(i):
-        for event, lag in ((e0, 0), (e1, LOOK), (e2, 2 * LOOK), (e3, 3 * LOOK)):
-            if 0 <= i - lag < len(gathers):
-                if lag == 0:
-                    ready(i)
-                event(gathers[i - lag])
-
-    for i in range(3):
-        gather(i)
+    done = []
+
+    def ahead(count):
+        for i in range(len(done), count + 1):
+            done.append(i)
+            for event, lag in ((e0, 0), (e1, LOOK), (e2, 2 * LOOK)):
+                if 0 <= i - lag < len(gathers):
+                    if lag == 0:
+                        ready(i)
+                    event(gathers[i - lag])
+
+    def arrive(i, lag):
+        ahead(i + lag)
+        e3(gathers[i])
+
+    ahead(2)
 
     for edge, k in ((0, 0), (3, 2)):
 
@@ -410,8 +422,7 @@
     s.mask[0:384, 384:768] = as_bias(seen)
     s.mask[384:768, 384:768] = as_bias(causal & (seg_wide == seg_tall))
 
-    for i in range(3, 3 * LOOK + 1):
-        gather(i)
+    arrive(0, LAG_IN)
 
     def tile_sum(q):
         total = jnp.zeros((16, 128), F32)
@@ -455,7 +466,7 @@
         s.qkv[section, 2 * n + 1] = mixed[:, 128:256]
 
     for part in range(6):
-        gather(3 * LOOK + 1 + part)
+        arrive(1 + part, LAG_IN)
         project(part)
 
     factor = HD**-0.5 * LOG2E
@@ -492,7 +503,10 @@
 
     for j in range(4):
         pre[8 + j].wait_send()
-    lax.fori_loop(0, 4, attend, 0)
+    lax.fori_loop(0, 2, attend, 0)
+    ahead(6 + LAG_IN + 1)
+    lax.fori_loop(2, 4, attend, 0)
+    ahead(6 + LAG_IN + 2)
 
     my_half = pl.ds(pl.multiple_of(r * 512, 512), 512)
     o_half = pl.ds(pl.multiple_of(o * 512, 512), 512)
@@ -504,7 +518,7 @@
     core_copy(1, s.half_t.at[o], s.att_t.at[my_half]).start()
     s.wide[:, my_half] = s.half[r]
     s.att_t[my_half] = s.half_t[r]
-    gather(3 * LOOK + 7)
+    arrive(7, LAG_FF)
     out_swap = core_copy(2, s.wout.at[:, :, :, r], s.wout.at[:, :, :, r])
     out_swap.start()
     core_copy(0, s.wide.at[:, o_half], s.wide.at[:, o_half]).wait_recv()
@@ -547,7 +561,7 @@
         )
 
     def rs_in(i):
-        slot, part = ((0, 0), (1, 0), (0, 1), (1, 1), (2, 0), (2, 1))[i]
+        slot, part = ((0, 0), (0, 1), (1, 0), (1, 1), (2, 0), (2, 1))[i]
         half = slice(256 * part, 256 * part + 256)
         return Bag(
             t=9 + i, fin=4 + i, split=False, piece=lambda a, b, c: s.win.at[i, a, b, c],
@@ -770,9 +784,18 @@
             if 0 <= i - lag < len(order):
                 event(order[i - lag])
 
+    stepped = []
+
+    def next_step():
+        step(len(stepped))
+        stepped.append(True)
+
     def feed(j, between):
-        gather(3 * LOOK + 8 + 2 * j)
-        gather(3 * LOOK + 9 + 2 * j)
+        if j == 3 and EARLY_CHUNK == 3:
+            for it in order[:LEAD]:
+                f0(it)
+        arrive(8 + 2 * j, LAG_FF)
+        arrive(9 + 2 * j, LAG_FF)
         sent(gathers[8 + 2 * j])
         sent(gathers[9 + 2 * j])
         between(0)
@@ -803,6 +826,10 @@
             s.bn_acc[:, :, cols] += back.reshape(2, 384, 256)
             return inside
 
+        ahead(9 + 2 * j + LAG_FF + 1)
+        if j == EARLY_CHUNK == 2:
+            for it in order[:LEAD]:
+                f0(it)
         lax.fori_loop(0, 4, wide_tile, 0)
         between(1)
 
@@ -828,14 +855,12 @@
 
     def start_reduction(place_in):
         if place_in == 0:
-            for it in order[:LEAD]:
-                f0(it)
-            step(0)
+            next_step()
         elif place_in == 1:
             core_copy(4, s.bn_acc.at[o], s.cross).start()
-            step(1)
+            next_step()
         else:
-            step(2)
+            next_step()
 
     feed(3, start_reduction)
 
@@ -879,7 +904,7 @@
     lax.fori_loop(0, 4, back_att, 0)
     core_copy(6, s.half.at[o], s.ba_all.at[r]).start()
     s.ba_all[r] = s.half[r]
-    step(3)
+    next_step()
     sent(gathers[7])
 
     def grad_out(n, carry):
@@ -938,9 +963,9 @@
     lax.fori_loop(0, 4, add_out, 0)
 
     lax.fori_loop(0, 1, attend_back, 0)
-    step(4)
+    next_step()
     lax.fori_loop(1, 3, attend_back, 0)
-    step(5)
+    next_step()
     lax.fori_loop(3, 4, attend_back, 0)
 
     core_copy(5, s.n_all.at[o], s.n_all.at[o]).wait_send()
@@ -956,16 +981,16 @@
 
     lax.fori_loop(0, 4, back_in, 0)
     core_copy(8, s.out_acc.at[o], s.cross).start()
-    step(6)
+    next_step()
     for part in range(6):
         sent(gathers[1 + part])
         at = (part % 2) * 256
         grad = dot(s.n1t[...], s.ffb[part // 2, :, at : at + 256]).astype(BF)
         s.win[part] = grad.reshape(4, 2, 2, 64, 256)
         if part == 2:
-            step(7)
-    step(8)
-    step(9)
+            next_step()
+    next_step()
+    next_step()
 
     core_copy(8, s.out_acc.at[o], s.cross).wait_recv()
 
@@ -998,8 +1023,8 @@
                 chunk = [s.gexp[j, 0:1, block] for j in range(4)]
                 s.sg[zz, yy, xx, 8:9] = pick([chunk[(q - g) % 4] for g in range(4)], group_1)
 
-    for i in range(10, len(order) + 5):
-        step(i)
+    while len(stepped) < len(order) + 5:
+        next_step()
 
     for i, item in enumerate(pre):
         if not 8 <= i < 12:

time: 243 us -> 232 us (0.955)
  Pallas kernels: 236 us -> 225 us
    pallas_call x1, Pallas kernels: 234 us -> 222 us  [fused_shards(): pl.pallas_call(functools.partial(layer_kernel, tuple(scratch)), out_shape...]
where the time goes in v4:
time: 232 us; the launch traced here: 231 us
  Pallas kernels  225 us (97%)
  local copies, waits for them, and re-layouts  3.29 us (1%)
    pallas_call x1, Pallas kernels, fused_shards(): pl.pallas_call(functools.partial(layer_kernel, tuple(scratch)), out_shape...  222 us

profile of v4, /device:TPU:1, one launch (start us, length us, event | category | flops | bytes accessed | tf_op | source)
XLA Modules:
  0.0 231.4 jit_solution(2058734560056798084)
XLA Ops:
  2.0 0.0 copy-start.9
  2.0 0.0 copy-start.5
  2.0 0.0 copy-start.6
  2.0 0.0 copy-start.7
  2.0 0.0 copy-start.8
  2.0 0.0 copy-start.2
  2.1 0.0 copy-start.3
  2.1 0.0 copy-start.4
  2.1 0.1 pad.2.clone
  2.2 0.5 copy-done.9
  2.6 0.0 copy-done.5
  2.6 0.0 copy-done.6
  2.7 0.0 copy-done.7
  2.7 0.0 copy-done.8
  2.7 0.0 copy-done.2
  2.7 0.0 copy-done.3
  2.7 0.0 copy-done.4
  2.8 0.1 tile.10
  2.9 0.0 copy-start.1
  2.9 0.6 copy-done.1
  3.5 0.7 maximum_maximum_fusion.refs_5_
  4.2 222.5 %shard_map.289 = (bf16[384,1024]{1,0:T(8,128)(2,1)}, bf16[384,1024]{1,0:T(8,128)(2,1)}, f32[32,3072]{1,0:T(8,128)}, f32[32,1024]{1,0:T(8,128)}, f32[32,4096]{1,0...) custom-call(s32[1]{0:T(128)S(6)} %copy.33.refs_0_, s32[1]{0:T(128)S(6)} %copy.34.refs_1_, s32[1,384]{1,0:T(1,128)} %refs_2_.1, ...), custom_call_target="tpu_custom_call" | custom-call | tf_op jit(solution)/shard_map/pallas_call | solution.py:1074
  226.7 2.9 %shard_map.290 = (bf16[384,1024]{1,0:T(8,128)(2,1)}, bf16[384,1024]{1,0:T(8,128)(2,1)}, f32[32,3072]{1,0:T(8,128)}, f32[32,1024]{1,0:T(8,128)}, f32[32,4096]{1,0:T(8,128)}, /*index=5*/f32[128,1024]{1,0:T(8,128)}) custom-call(bf16[384,1024]{1,0:T(8,128)(2,1)} %get-tuple-element.28.refs_0_, bf16[384,1024]{1,0:T(8,128)(2,1)} %get-tuple-element.29.refs_1_, ...), custom_call_target="tpu_custom_call" | custom-call | tf_op jit(solution)/shard_map/pallas_call | solution.py:1096
  229.6 0.0 copy-start
  229.6 0.7 copy-done
  230.3 0.5 slice_bitcast_fusion.1
  230.8 0.1 constant_dynamic-slice_fusion
  230.8 0.5 slice_bitcast_fusion
  (5 shorter events, 0.1 us)
Async XLA Ops:
  2.0 0.7 copy-start.9
  2.0 0.7 copy-start.5
  2.0 0.7 copy-start.6
  2.0 0.7 copy-start.7
  2.0 0.7 copy-start.8
  2.0 0.7 copy-start.2
  2.1 0.7 copy-start.3
  2.1 0.7 copy-start.4
  2.9 0.7 copy-start.1
  229.6 0.7 copy-start

commit v5 on v4

--- a/solution.py
+++ b/solution.py
@@ -107,7 +107,7 @@
         fin_w_in=v((6, 32, 256), F32),
         sfin=v((16, 128), F32),
         sfin_in=v((16, 128), F32),
-        own_s=dma((2,)),
+        own_s=dma((7,)),
         pre_s=dma((13,)),
         pre_r=dma((13,)),
         agz_s=dma((16, 3)),
@@ -235,13 +235,16 @@
     own_cot = pltpu.make_async_copy(cot_ref, s.c_all.at[r], s.own_s.at[1])
     own_frames.start()
     own_cot.start()
+    own_more = [pltpu.make_async_copy(wout_in, s.wout.at[z, y, x, r], s.own_s.at[2])]
+    for j in range(4):
+        group = (place + 4 - j) % 4
+        rows = pl.ds(pl.multiple_of(group * 32, 32), 32)
+        own_more.append(pltpu.make_async_copy(wred_in.at[rows], s.wred.at[j, z, group], s.own_s.at[3 + j]))
+    for item in own_more:
+        item.start()
     s.small[z, y, x, r] = small_in[...]
     for i in range(6):
         s.win[i, z, y, x, my_rows] = win_in[:, part_cols(i, r)]
-    s.wout[z, y, x, r] = wout_in[...]
-    for j in range(4):
-        group = (place + 4 - j) % 4
-        s.wred[j, z, group] = wred_in[pl.ds(pl.multiple_of(group * 32, 32), 32)]
     for j in range(4):
         s.wexp[j, z, y, x, my_rows] = s.half[r, j * 32 : (j + 1) * 32]
 
@@ -406,6 +409,8 @@
 
     own_frames.wait()
     own_cot.wait()
+    for item in own_more:
+        item.wait()
     prefix = phon_ref[0] + prom_ref[0]
     seg_row = seg_ref[...].astype(F32)
     seg_wide = jnp.broadcast_to(seg_row, (384, 384))
@@ -777,7 +782,7 @@
     order = []
     for j in range(4):
         order += [rs_red(j), rs_exp(j)]
-    order += [rs_out()] + [rs_in(i) for i in range(6)] + [rs_small()]
+    order += [rs_out()] + [rs_in(i) for i in range(3)] + [rs_small()] + [rs_in(i) for i in range(3, 6)]
 
     def step(i):
         for event, lag in ((f0, -LEAD), (f1, 1), (f2, 2), (f3, 3), (f4, 4), (f5, 5)):
@@ -1040,12 +1045,18 @@
 
 
 def hand_on(*refs):
-    given, taken, held = refs[0:6], refs[6:12], refs[12:18]
-    sems = refs[18]
+    given, tile_ref, taken = refs[0:6], refs[6], refs[7:13]
+    vectors, held, sems = refs[13:22], refs[22:28], refs[28]
     inward = [pltpu.make_async_copy(given[i], held[i], sems.at[0, i]) for i in range(6)]
     outward = [pltpu.make_async_copy(held[i], taken[i], sems.at[1, i]) for i in range(6)]
     for item in inward:
         item.start()
+    quarter = (lax.axis_index("dp") * 2 + lax.axis_index("role")) % 4
+    tile = tile_ref[...]
+    turned = pltpu.roll(tile, (4 - quarter) % 4 * 32, 1)
+    for row in range(8):
+        vectors[row][...] = turned[row, 0:32]
+    vectors[8][...] = tile[8]
     for i in range(6):
         inward[i].wait()
         outward[i].start()
@@ -1082,7 +1093,7 @@
             jax.ShapeDtypeStruct((128, 1024), F32),
             jax.ShapeDtypeStruct((16, 128), F32),
         ],
-        in_specs=[smem, smem, vmem, hbm, hbm] + [vmem] * 5,
+        in_specs=[smem, smem, vmem, hbm, hbm, vmem, vmem, hbm, vmem, hbm],
         out_specs=[vmem] * 7,
         scratch_shapes=list(scratch.values()),
         compiler_params=pltpu.CompilerParams(
@@ -1092,19 +1103,21 @@
         phoneme_len, prompt_len, target_segment, frames[0], frames_cotangent[0], small, inward_weight,
         outward_weight, expand_weight, reduce_weight,
     )
-    d_small = outs[6]
-    result, frames_gradient, d_in, d_out, d_exp, d_red = pl.pallas_call(
+    *moved, = pl.pallas_call(
         hand_on,
-        out_shape=[jax.ShapeDtypeStruct(item.shape, item.dtype) for item in outs[:6]],
-        in_specs=[hbm] * 6,
-        out_specs=[hbm] * 6,
+        out_shape=[jax.ShapeDtypeStruct(item.shape, item.dtype) for item in outs[:6]]
+        + [jax.ShapeDtypeStruct((32,), F32)] * 8
+        + [jax.ShapeDtypeStruct((128,), F32)],
+        in_specs=[hbm] * 6 + [vmem],
+        out_specs=[hbm] * 6 + [vmem] * 9,
         scratch_shapes=[pltpu.VMEM(item.shape, item.dtype) for item in outs[:6]]
         + [pltpu.SemaphoreType.DMA((2, 6))],
-    )(*outs[:6])
-    mine = lax.dynamic_slice(d_small, (0, quarter * 32), (8, 32))
+    )(*outs)
+    result, frames_gradient, d_in, d_out, d_exp, d_red = moved[:6]
+    mine, bias_row = moved[6:14], moved[14]
     return (
         result[None], frames_gradient[None], mine[0], mine[1], d_in, mine[2], mine[3], d_out, mine[4], mine[5],
-        mine[6], d_exp, d_small[8], d_red, mine[7],
+        mine[6], d_exp, bias_row, d_red, mine[7],
     )
 
 

time: 232 us -> 230 us (level)
  no operation moved by 1% of the time
where the time goes in v5:
time: 230 us
  Pallas kernels  226 us (98%)
    pallas_call x1, Pallas kernels, fused_shards(): pl.pallas_call(functools.partial(layer_kernel, tuple(scratch)), out_shape...  222 us

profile of v5, /device:TPU:1, one launch (start us, length us, event | category | flops | bytes accessed | tf_op | source)
XLA Modules:
  0.0 230.3 jit_solution(7683156087361235387)
XLA Ops:
  2.0 0.0 copy-start.8
  2.0 0.0 copy-start.4
  2.0 0.0 copy-start.5
  2.0 0.0 copy-start.6
  2.0 0.0 copy-start.7
  2.0 0.0 copy-start.1
  2.0 0.0 copy-start.2
  2.1 0.0 copy-start.3
  2.1 0.1 pad.2.clone
  2.1 0.5 copy-done.8
  2.6 0.0 copy-done.4
  2.6 0.0 copy-done.5
  2.7 0.0 copy-done.6
  2.7 0.0 copy-done.7
  2.7 0.0 copy-done.1
  2.7 0.0 copy-done.2
  2.7 0.0 copy-done.3
  2.8 0.1 tile.10
  2.9 0.0 copy-start
  2.9 0.6 copy-done
  3.5 0.7 maximum_maximum_fusion.refs_5_
  4.2 221.7 %shard_map.289 = (bf16[384,1024]{1,0:T(8,128)(2,1)}, bf16[384,1024]{1,0:T(8,128)(2,1)}, f32[32,3072]{1,0:T(8,128)}, f32[32,1024]{1,0:T(8,128)}, f32[32,4096]{1,0...) custom-call(s32[1]{0:T(128)S(6)} %copy.33.refs_0_, s32[1]{0:T(128)S(6)} %copy.34.refs_1_, s32[1,384]{1,0:T(1,128)} %refs_2_.1, ...), custom_call_target="tpu_custom_call" | custom-call | tf_op jit(solution)/shard_map/pallas_call | solution.py:1085
  225.9 4.1 %shard_map.290 = (bf16[384,1024]{1,0:T(8,128)(2,1)}, bf16[384,1024]{1,0:T(8,128)(2,1)}, f32[32,3072]{1,0:T(8,128)}, f32[32,1024]{1,0:T(8,128)}, f32[32,4096]{1,0...) custom-call(bf16[384,1024]{1,0:T(8,128)(2,1)} %get-tuple-element.37., ...), custom_call_target="tpu_custom_call" | custom-call | tf_op jit(solution)/shard_map/pallas_call | solution.py:1106
  (5 shorter events, 0.1 us)
Async XLA Ops:
  2.0 0.7 copy-start.8
  2.0 0.7 copy-start.4
  2.0 0.7 copy-start.5
  2.0 0.7 copy-start.6
  2.0 0.7 copy-start.7
  2.0 0.7 copy-start.1
  2.0 0.7 copy-start.2
  2.1 0.7 copy-start.3
  2.9 0.7 copy-start

commit v6 on v5

--- a/solution.py
+++ b/solution.py
@@ -785,7 +785,7 @@
     order += [rs_out()] + [rs_in(i) for i in range(3)] + [rs_small()] + [rs_in(i) for i in range(3, 6)]
 
     def step(i):
-        for event, lag in ((f0, -LEAD), (f1, 1), (f2, 2), (f3, 3), (f4, 4), (f5, 5)):
+        for event, lag in ((f0, -LEAD), (f1, 1), (f2, 2), (f3, 3), (f4, 5), (f5, 6)):
             if 0 <= i - lag < len(order):
                 event(order[i - lag])
 
@@ -1028,7 +1028,7 @@
                 chunk = [s.gexp[j, 0:1, block] for j in range(4)]
                 s.sg[zz, yy, xx, 8:9] = pick([chunk[(q - g) % 4] for g in range(4)], group_1)
 
-    while len(stepped) < len(order) + 5:
+    while len(stepped) < len(order) + 6:
         next_step()
 
     for i, item in enumerate(pre):

time: 230 us -> 230 us (level)
  no operation moved by 1% of the time
where the time goes in v6:
time: 230 us
  Pallas kernels  226 us (98%)
    pallas_call x1, Pallas kernels, fused_shards(): pl.pallas_call(functools.partial(layer_kernel, tuple(scratch)), out_shape...  221 us

profile of v6, /device:TPU:1, one launch (start us, length us, event | category | flops | bytes accessed | tf_op | source)
XLA Modules:
  0.0 229.9 jit_solution(2794453670008056700)
XLA Ops:
  2.0 0.0 copy-start.8
  2.0 0.0 copy-start.4
  2.0 0.0 copy-start.5
  2.0 0.0 copy-start.6
  2.0 0.0 copy-start.7
  2.0 0.0 copy-start.1
  2.0 0.0 copy-start.2
  2.1 0.0 copy-start.3
  2.1 0.1 pad.2.clone
  2.1 0.5 copy-done.8
  2.6 0.0 copy-done.4
  2.6 0.0 copy-done.5
  2.7 0.0 copy-done.6
  2.7 0.0 copy-done.7
  2.7 0.0 copy-done.1
  2.7 0.0 copy-done.2
  2.7 0.0 copy-done.3
  2.8 0.1 tile.10
  2.9 0.0 copy-start
  2.9 0.6 copy-done
  3.5 0.7 maximum_maximum_fusion.refs_5_
  4.2 221.4 %shard_map.289 = (bf16[384,1024]{1,0:T(8,128)(2,1)}, bf16[384,1024]{1,0:T(8,128)(2,1)}, f32[32,3072]{1,0:T(8,128)}, f32[32,1024]{1,0:T(8,128)}, f32[32,4096]{1,0...) custom-call(s32[1]{0:T(128)S(6)} %copy.33.refs_0_, s32[1]{0:T(128)S(6)} %copy.34.refs_1_, s32[1,384]{1,0:T(1,128)} %refs_2_.1, ...), custom_call_target="tpu_custom_call" | custom-call | tf_op jit(solution)/shard_map/pallas_call | solution.py:1085
  225.6 4.1 %shard_map.290 = (bf16[384,1024]{1,0:T(8,128)(2,1)}, bf16[384,1024]{1,0:T(8,128)(2,1)}, f32[32,3072]{1,0:T(8,128)}, f32[32,1024]{1,0:T(8,128)}, f32[32,4096]{1,0...) custom-call(bf16[384,1024]{1,0:T(8,128)(2,1)} %get-tuple-element.37., ...), custom_call_target="tpu_custom_call" | custom-call | tf_op jit(solution)/shard_map/pallas_call | solution.py:1106
  (5 shorter events, 0.1 us)
Async XLA Ops:
  2.0 0.7 copy-start.8
  2.0 0.7 copy-start.4
  2.0 0.7 copy-start.5
  2.0 0.7 copy-start.6
  2.0 0.7 copy-start.7
  2.0 0.7 copy-start.1
  2.0 0.7 copy-start.2
  2.1 0.7 copy-start.3
  2.9 0.7 copy-start
